TPU v7x, 32 devices: a whole 2x2x4 slice. The times are simulated.
32 devices in a mesh: rep: 16 (over z, y, x), shard: 2 (over core).
Axes of the slice: x: 2, y: 2, z: 4, core: 2. Of those that a mesh axis runs over, the one named last changes fastest.
Arguments:
- hidden: bfloat16 [16, 1024, 768], P('rep', 'shard'), may hold values from -6 to 6
- latents: bfloat16 [16, 6, 768], P('rep'), may hold values from -6 to 6
- latent_pos: int32 [16, 6], P('rep'), may hold values from 0 to 1023, as said below
- prefix: int32 [16], P('rep'), may hold values from 102 to 512
- ln1_gain: bfloat16 [768], P('shard'), may hold values from 0.099609375 to 1.8984375
- ln1_bias: bfloat16 [768], P('shard'), may hold values from -1.75 to 1.75
- w_qkv: bfloat16 [768, 2304], P('shard'), may hold values from -0.21875 to 0.21875
- b_qv: bfloat16 [1536], P('shard'), may hold values from -1.75 to 1.75
- w_proj: bfloat16 [768, 768], P('shard'), may hold values from -6 to 6
- b_proj: bfloat16 [768], P('shard'), may hold values from -1.75 to 1.75
- ln2_gain: bfloat16 [768], P('shard'), may hold values from 0.099609375 to 1.8984375
- ln2_bias: bfloat16 [768], P('shard'), may hold values from -1.75 to 1.75
- w_fc: bfloat16 [768, 3072], P('shard'), may hold values from -0.21875 to 0.21875
- b_fc: bfloat16 [3072], P('shard'), may hold values from -1.75 to 1.75
- w_out: bfloat16 [3072, 768], P('shard'), may hold values from -0.109375 to 0.109375
- b_out: bfloat16 [768], P('shard'), may hold values from -1.75 to 1.75
- cotangent: bfloat16 [16, 1024, 768], P('rep', 'shard'), may hold values from -6 to 6
Outputs:
- block_out: bfloat16 [16, 1024, 768], P('rep', 'shard')
- grad_hidden: bfloat16 [16, 1024, 768], P('rep', 'shard')
- grad_latents: float32 [16, 6, 768], P('rep')
- grad_ln1_gain: float32 [768], P('shard')
- grad_ln1_bias: float32 [768], P('shard')
- grad_w_qkv: float32 [768, 2304], P('shard')
- grad_b_qv: float32 [1536], P('shard')
- grad_w_proj: float32 [768, 768], P('shard')
- grad_b_proj: float32 [768], P('shard')
- grad_ln2_gain: float32 [768], P('shard')
- grad_ln2_bias: float32 [768], P('shard')
- grad_w_fc: float32 [768, 3072], P('shard')
- grad_b_fc: float32 [3072], P('shard')
- grad_w_out: float32 [3072, 768], P('shard')
- grad_b_out: float32 [768], P('shard')
Inputs may be any that keep to these rules, and one draw needn't show every extreme that they name: `latent_pos`: the 6 positions of one sequence are distinct.
All inputs are finite; a program needn't handle non-finite values.
Results may differ from a plain program's by a relative error of at most 0.018.
Values may be sent and summed in bfloat16 or wider, within the bound.
No kernel may reach another device: no remote copies, remote signals or barrier semaphores. Data moves between devices by JAX's collectives and lax.ppermute only.
A program may use at most 256 MiB of HBM per device.

v0:
```python
import functools
import jax
import jax.numpy as jnp
from jax import lax
from jax.experimental import pallas as pl
from jax.experimental.pallas import tpu as pltpu
from jax.sharding import PartitionSpec as P

HEADS = 12
F32 = jnp.float32
BF = jnp.bfloat16

norm_epsilon = 1e-05
gelu_root = 0.7978845608028654
gelu_cubic = 0.044715
masked_score = -1e30
LOG2E = 1.4426950408889634


def dot_nt(a, b):
    return lax.dot_general(a, b, (((1,), (1,)), ((), ())), preferred_element_type=F32)


def dot_nn(a, b):
    return lax.dot_general(a, b, (((1,), (0,)), ((), ())), preferred_element_type=F32)


def dot_tn(a, b):
    return lax.dot_general(a, b, (((0,), (0,)), ((), ())), preferred_element_type=F32)


def params(semantics=None, mb=16):
    return pltpu.CompilerParams(dimension_semantics=semantics, vmem_limit_bytes=mb * 1024 * 1024)


def cost(flops, nbytes, trans=0):
    return pl.CostEstimate(flops=1, bytes_accessed=1, transcendentals=0)


def whole(shape):
    return pl.BlockSpec(shape, lambda *_: (0,) * len(shape), pipeline_mode=pl.Buffered(1))


def both(own, oth, shard, a, n):
    o = own[0:1, a : a + n].astype(F32)
    t = oth[0:1, a : a + n].astype(F32)
    first = jnp.where(shard == 0, o, t)
    second = jnp.where(shard == 0, t, o)
    return jnp.concatenate([first, second], axis=1)


def half(i, n):
    return pl.ds(pl.multiple_of(i * n, n), n)


def call(kernel, name, grid, in_specs, out_specs, out_shape, scratch, est, args, mb=16):
    return pl.pallas_call(
        kernel,
        out_shape=out_shape,
        grid_spec=pltpu.PrefetchScalarGridSpec(
            num_scalar_prefetch=1, grid=grid, in_specs=in_specs, out_specs=out_specs, scratch_shapes=scratch
        ),
        compiler_params=params(("arbitrary",), mb),
        cost_estimate=est,
        name=name,
    )(*args)


sds = jax.ShapeDtypeStruct


def pack(vecs):
    n = sum(v.shape[0] for v in vecs)
    at = 0
    out = []
    for v in vecs:
        out.append(jnp.pad(v, (at, n - at - v.shape[0])))
        at += v.shape[0]
    return functools.reduce(jnp.add, out)[None, :]


def qv_bias(pk_own, pk_oth, shard, which, heads):
    H = pk_own.shape[1] // 12
    a = pk_own[0:1, 2 * H : 4 * H].astype(F32)
    b = pk_oth[0:1, 2 * H : 4 * H].astype(F32)
    src = jnp.where(shard == which, a, b)
    return jnp.where(heads == 0, src[:, :H], src[:, H:])


def project(n, ws, pk_own, pk_oth, shard, heads, out):
    H = ws.shape[0] // 2
    for j in range(3):
        y = dot_nn(n, ws[:, j * H : (j + 1) * H])
        if j != 1:
            y = y + qv_bias(pk_own, pk_oth, shard, j // 2, heads)
        out[:, j * H : (j + 1) * H] = y.astype(BF)


def ln_send_kernel(
    scal, hid, lat, pk_own, pk_oth, qo, ko, vo, qt, kt, vt, send, normed, nrm_send, xb, xs, ns, ws, *, L
):
    r = pl.program_id(0)
    RB, D = hid.shape
    H = D // 2
    shard = scal[0]

    @pl.when(r == 0)
    def _():
        for j, (o, t) in enumerate(((qo, qt), (ko, kt), (vo, vt))):
            ws[half(shard, H), j * H : (j + 1) * H] = o[...]
            ws[half(1 - shard, H), j * H : (j + 1) * H] = t[...]

    xs[...] = hid[...].astype(F32)
    row0 = shard * L + r * RB
    for c in range(6):
        rel = scal[2 + c] - row0

        @pl.when((rel >= 0) & (rel < RB))
        def _():
            xs[pl.ds(rel, 1), :] = lat[c : c + 1, :].astype(F32)

    g = both(pk_own, pk_oth, shard, 0, H)
    b = both(pk_own, pk_oth, shard, H, H)
    x = xs[...]
    xb[...] = x.astype(BF)
    cen = x - jnp.mean(x, axis=1, keepdims=True)
    var = jnp.mean(cen * cen, axis=1, keepdims=True)
    n = (cen * lax.rsqrt(var + norm_epsilon) * g + b).astype(BF)
    ns[...] = n
    normed[...] = n
    nrm_send[...] = ns[:, half(1 - shard, H)]
    project(n, ws, pk_own, pk_oth, shard, 1 - shard, send)


def ln_send(scal, hid, lat, pk_own, pk_oth, w_own, w_oth):
    L, D = hid.shape
    H = D // 2
    RB = L // 2
    NP = pk_own.shape[1]
    rows = lambda n: pl.BlockSpec((RB, n), lambda r, s: (r, 0))
    w = [
        pl.BlockSpec((H, H), lambda r, s, j=j: (0, 2 * j + 1 - s[0]), pipeline_mode=pl.Buffered(1)) for j in range(3)
    ]
    return call(
        functools.partial(ln_send_kernel, L=L), "ln_send", (2,),
        [rows(D), whole(lat.shape), whole((1, NP)), whole((1, NP))] + w + w,
        [rows(3 * H), rows(D), rows(H), rows(D)],
        (sds((L, 3 * H), BF), sds((L, D), BF), sds((L, H), BF), sds((L, D), BF)),
        [pltpu.VMEM((RB, D), F32), pltpu.VMEM((RB, D), BF), pltpu.VMEM((D, 3 * H), BF)],
        cost(6 * L * D * H, 6e6),
        (scal, hid, lat, pk_own, pk_oth, w_own, w_own, w_own, w_oth, w_oth, w_oth),
    )


def own_kernel(scal, normed, pk_own, pk_oth, qo, ko, vo, qt, kt, vt, keep, ws):
    H = qo.shape[0]
    shard = scal[0]

    @pl.when(pl.program_id(0) == 0)
    def _():
        for j, (o, t) in enumerate(((qo, qt), (ko, kt), (vo, vt))):
            ws[half(shard, H), j * H : (j + 1) * H] = o[...]
            ws[half(1 - shard, H), j * H : (j + 1) * H] = t[...]

    project(normed[...], ws, pk_own, pk_oth, shard, shard, keep)


def own_heads(scal, normed, pk_own, pk_oth, w_own, w_oth):
    L, D = normed.shape
    H = D // 2
    RB = L // 2
    NP = pk_own.shape[1]
    rows = lambda n: pl.BlockSpec((RB, n), lambda r, s: (r, 0))
    w = [pl.BlockSpec((H, H), lambda r, s, j=j: (0, 2 * j + s[0]), pipeline_mode=pl.Buffered(1)) for j in range(3)]
    return call(
        own_kernel, "own_heads", (2,),
        [rows(D), whole((1, NP)), whole((1, NP))] + w + w, rows(3 * H), sds((L, 3 * H), BF),
        [pltpu.VMEM((D, 3 * H), BF)],
        cost(6 * L * D * H, 4e6),
        (scal, normed, pk_own, pk_oth, w_own, w_own, w_own, w_oth, w_oth, w_oth),
    )


def join(dst, own, oth, shard):
    L = own.shape[0]
    dst[half(shard, L), :] = own[...]
    dst[half(1 - shard, L), :] = oth[...]


def attn_fwd_kernel(scal, qa, ka, va, qb, kb_, vb, o_keep, o_send, lse_ref, qs, ks, vs, os_, stat, *, L, RB):
    p_id = pl.program_id(0)
    shard = scal[0]
    pfx = scal[1]
    join(qs, qa, qb, shard)
    join(ks, ka, kb_, shard)
    join(vs, va, vb, shard)
    lane = lax.broadcasted_iota(jnp.int32, (RB, 128), 1)
    c = 0.125 * LOG2E
    HB = L // RB

    for r in range(2 * HB):
        q = qs[r * RB : (r + 1) * RB, :]
        outs = []
        for hh in range(2):
            sel = (lane < 64) if hh == 0 else (lane >= 64)
            qm = jnp.where(sel, q, jnp.zeros_like(q))
            pieces = []
            if r >= HB:
                pieces.append((dot_nt(qm, ks[0:L, :]) * c, vs[0:L, :]))
            for kb in range(HB) if r < HB else range(HB, r + 1):
                s = dot_nt(qm, ks[kb * RB : (kb + 1) * RB, :]) * c
                if kb >= r:
                    col = lax.broadcasted_iota(jnp.int32, (RB, RB), 1) + kb * RB
                    row = lax.broadcasted_iota(jnp.int32, (RB, RB), 0) + r * RB
                    keep = (col <= row) | (col < pfx) if r < HB else (col <= row)
                    s = jnp.where(keep, s, masked_score)
                pieces.append((s, vs[kb * RB : (kb + 1) * RB, :]))
            m = functools.reduce(jnp.maximum, [jnp.max(s, axis=1, keepdims=True) for s, _ in pieces])
            total = jnp.zeros((RB, 1), F32)
            o = jnp.zeros((RB, 128), F32)
            for s, v in pieces:
                p = jnp.exp2(s - m)
                total = total + jnp.sum(p, axis=1, keepdims=True)
                o = o + dot_nn(p.astype(BF), v)
            outs.append(o * (1.0 / total))
            lse = m + jnp.log2(total)
            here = lane == p_id * 2 + hh
            stat[r * RB : (r + 1) * RB, :] = jnp.where(here, lse, stat[r * RB : (r + 1) * RB, :])
        os_[r * RB : (r + 1) * RB, :] = jnp.where(lane < 64, outs[0], outs[1]).astype(BF)

    o_keep[...] = os_[half(shard, L), :]
    o_send[...] = os_[half(1 - shard, L), :]

    @pl.when(p_id == pl.num_programs(0) - 1)
    def _():
        lse_ref[...] = stat[...].T[0:8, :]


def attn_fwd(scal, keep, recv):
    L, W = keep.shape
    H = W // 3
    NP = H // 128
    spec = lambda off: pl.BlockSpec((L, 128), lambda p, s: (0, p + off))
    seq = pltpu.VMEM((2 * L, 128), BF)
    o = sds((L, H), BF)
    return call(
        functools.partial(attn_fwd_kernel, L=L, RB=256), "attn_fwd", (NP,),
        [spec(0), spec(NP), spec(2 * NP)] * 2,
        [spec(0), spec(0), pl.BlockSpec((8, 2 * L), lambda p, s: (0, 0))],
        (o, o, sds((8, 2 * L), F32)),
        [seq, seq, seq, seq, pltpu.VMEM((2 * L, 128), F32)],
        cost(12e9, 4e6, 6e6),
        (scal, keep, keep, keep, recv, recv, recv),
    )


def attn_bwd_kernel(
    scal, qa, ka, va, qb, kb_, vb, ga, gb, aa, ab, lse_ref, d_own, d_oth, qs, ks, vs, gs, as_, dks, dvs, dqt, *, L, KB, p0
):
    shard = scal[0]
    pfx = scal[1]
    join(qs, qa, qb, shard)
    join(ks, ka, kb_, shard)
    join(vs, va, vb, shard)
    join(gs, ga, gb, shard)
    join(as_, aa, ab, shard)
    S = 2 * L
    c = 0.125 * LOG2E
    lane = lax.broadcasted_iota(jnp.int32, (S, 128), 1)
    q = qs[...]
    do = gs[...]
    z = jnp.zeros_like(q)
    qm = [jnp.where(lane < 64, q, z), jnp.where(lane >= 64, q, z)]
    dm = [jnp.where(lane < 64, do, z), jnp.where(lane >= 64, do, z)]
    prod = do.astype(F32) * as_[...].astype(F32)
    hi = prod.astype(BF)
    lo = (prod - hi.astype(F32)).astype(BF)
    head = lax.broadcasted_iota(jnp.int32, (16, 128), 0)
    plane = lax.broadcasted_iota(jnp.int32, (16, 128), 1)
    pick = jnp.where((plane >= head * 64) & (plane < head * 64 + 64), 1.0, 0.0).astype(BF)
    delta = dot_nt(pick, hi) + dot_nt(pick, lo)
    hb = (pl.program_id(0) + p0) * 2
    lse = [lse_ref[pl.ds(hb + hh, 1), :] for hh in range(2)]
    dl = [delta[hh : hh + 1, :] for hh in range(2)]
    dqt[...] = jnp.zeros_like(dqt)

    for kb in range(S // KB):
        rows = slice(kb * KB, (kb + 1) * KB)
        k = ks[rows, :]
        v = vs[rows, :]
        kt = k.T
        dk = None
        dv = None
        spans = [(0, L), (L, S)] if kb * KB < L else [(kb * KB, S)]
        for q0, q1 in spans:
            mask = None
            if q0 <= kb * KB:
                key = lax.broadcasted_iota(jnp.int32, (KB, q1 - q0), 0) + kb * KB
                qry = lax.broadcasted_iota(jnp.int32, (KB, q1 - q0), 1) + q0
                mask = (key <= qry) | (key < pfx) if q1 <= L else key <= qry
            for hh in range(2):
                st = dot_nt(k, qm[hh][q0:q1, :]) * c
                if mask is not None:
                    st = jnp.where(mask, st, masked_score)
                pt = jnp.exp2(st - lse[hh][:, q0:q1])
                dpt = dot_nt(v, dm[hh][q0:q1, :])
                dst = (pt * (dpt - dl[hh][:, q0:q1])).astype(BF)
                a = dot_nn(pt.astype(BF), dm[hh][q0:q1, :])
                b = dot_nn(dst, qm[hh][q0:q1, :])
                dv = a if dv is None else dv + a
                dk = b if dk is None else dk + b
                dqt[hh * 64 : (hh + 1) * 64, q0:q1] += dot_nn(kt[hh * 64 : (hh + 1) * 64, :], dst)
        dks[rows, :] = (dk * 0.125).astype(BF)
        dvs[rows, :] = dv.astype(BF)

    gs[...] = (dqt[...].T * 0.125).astype(BF)
    for j, src in enumerate((gs, dks, dvs)):
        d_own[j] = src[half(shard, L), :]
        d_oth[j] = src[half(1 - shard, L), :]


def attn_bwd(scal, keep, recv, ga_keep, ga_recv, att_keep, att_send, lse, p0, count):
    L, W = keep.shape
    H = W // 3
    NP = H // 128
    spec = lambda off: pl.BlockSpec((L, 128), lambda p, s: (0, p + off))
    seq = pltpu.VMEM((2 * L, 128), BF)
    o = sds((3, L, count * 128), BF)
    ospec = pl.BlockSpec((3, L, 128), lambda p, s: (0, 0, p))
    share = count / NP
    return call(
        functools.partial(attn_bwd_kernel, L=L, KB=256, p0=p0), "attn_bwd", (count,),
        [spec(p0), spec(NP + p0), spec(2 * NP + p0)] * 2 + [spec(p0)] * 4 + [pl.BlockSpec((8, 2 * L), lambda p, s: (0, 0))],
        [ospec, ospec], (o, o),
        [seq] * 7 + [pltpu.VMEM((128, 2 * L), F32)],
        cost(24e9 * share, 8e6 * share, 6e6 * share),
        (scal, keep, keep, keep, recv, recv, recv, ga_keep, ga_recv, att_keep, att_send, lse),
    )


def ffn_kernel(
    scal, ak, ar, xb, dz, pk_own, pk_oth, wp_own, wp_oth, wf_own, wf_oth, wo_own, wo_oth,
    act_keep, act_send, gp, n2_keep, n2_send, out, dmid, gb, ga_keep, ga_send, sfc, sums,
    ns, mid, yacc, gacc, wfs, wos, as_, *, T,
):
    t = pl.program_id(0)
    last = pl.num_programs(0) - 1
    NH = pl.num_programs(0) // 2
    shard = scal[0]
    L, D = xb.shape
    H = D // 2
    FH = wo_own.shape[0] * NH
    o_bp, o_g2, o_b2, o_bf = 4 * H, 5 * H, 6 * H, 7 * H
    o_bo = 11 * H
    RB = L // 4

    @pl.when(t == 0)
    def _():
        g = both(pk_own, pk_oth, shard, o_g2, H)
        b = both(pk_own, pk_oth, shard, o_b2, H)
        bp = both(pk_own, pk_oth, shard, o_bp, H)
        mid[...] = dot_nn(ak[...], wp_own[...]) + dot_nn(ar[...], wp_oth[...])
        for i in range(4):
            rows = slice(i * RB, (i + 1) * RB)
            m = mid[rows, :] + xb[rows, :].astype(F32) + bp
            mid[rows, :] = m
            cen = m - jnp.mean(m, axis=1, keepdims=True)
            var = jnp.mean(cen * cen, axis=1, keepdims=True)
            ns[rows, :] = (cen * lax.rsqrt(var + norm_epsilon) * g + b).astype(BF)
        n2_keep[...] = ns[:, half(shard, H)]
        n2_send[...] = ns[:, half(1 - shard, H)]
        yacc[...] = jnp.zeros_like(yacc)
        gacc[...] = jnp.zeros_like(gacc)

    wfs[half(shard, H), :] = wf_own[...]
    wfs[half(1 - shard, H), :] = wf_oth[...]

    @pl.when(t < NH)
    def _():
        wos[...] = wo_own[...]

    @pl.when(t >= NH)
    def _():
        wos[...] = wo_oth[...]

    at = pl.ds(pl.multiple_of(o_bf + lax.rem(t, NH) * T, 128), T)
    bias = jnp.where(t < NH, pk_own[0:1, at].astype(F32), pk_oth[0:1, at].astype(F32))
    CB = T // 2
    for i in range(2):
        cols = slice(i * CB, (i + 1) * CB)
        u = dot_nn(ns[...], wfs[:, cols]) + bias[:, cols]
        ga = dot_nt(dz[...], wos[cols, :])
        u2 = u * u
        th = jnp.tanh(u * (gelu_root + (gelu_root * gelu_cubic) * u2))
        hp = 0.5 + 0.5 * th
        av = u * hp
        slope = hp + av * ((1.0 - th) * (gelu_root + (3.0 * gelu_root * gelu_cubic) * u2))
        as_[:, cols] = av.astype(BF)
        g = (ga * slope).astype(BF)
        gp[:, cols] = g
        total = jnp.sum(g.astype(F32), axis=0, keepdims=True)
        sfc[:, cols] = jnp.broadcast_to(total, (sfc.shape[0], CB))
    yacc[...] += dot_nn(as_[...], wos[...])
    gacc[...] += dot_nt(gp[...], wfs[...])

    @pl.when(t < NH)
    def _():
        act_keep[...] = as_[...]

    @pl.when(t >= NH)
    def _():
        act_send[...] = as_[...]

    @pl.when(t == last)
    def _():
        g2 = both(pk_own, pk_oth, shard, o_g2, H)
        bo = both(pk_own, pk_oth, shard, o_bo, H)
        sums[...] = jnp.zeros_like(sums)
        for i in range(4):
            rows = slice(i * RB, (i + 1) * RB)
            m = mid[rows, :]
            out[rows, :] = (yacc[rows, :] + m + bo).astype(BF)
            gn = gacc[rows, :]
            cen = m - jnp.mean(m, axis=1, keepdims=True)
            r = lax.rsqrt(jnp.mean(cen * cen, axis=1, keepdims=True) + norm_epsilon)
            n = cen * r
            e = gn * g2
            dzv = dz[rows, :].astype(F32)
            g = dzv + r * (e - jnp.mean(e, axis=1, keepdims=True) - n * jnp.mean(e * n, axis=1, keepdims=True))
            dmid[rows, :] = g
            gbv = g.astype(BF)
            gb[rows, :] = gbv
            sums[0:1, :] += jnp.sum(gbv.astype(F32), axis=0, keepdims=True)
            sums[1:2, :] += jnp.sum(gn * n, axis=0, keepdims=True)
            sums[2:3, :] += jnp.sum(gn, axis=0, keepdims=True)
            sums[3:4, :] += jnp.sum(dzv, axis=0, keepdims=True)
        ga_keep[...] = dot_nt(gb[...], wp_own[...]).astype(BF)
        ga_send[...] = dot_nt(gb[...], wp_oth[...]).astype(BF)


def ffn(scal, ak, ar, xb, dz, pk_own, pk_oth, wp_own, wp_oth, wf_own, wf_oth, wo_own, wo_oth):
    L, D = xb.shape
    H = D // 2
    FH = wo_own.shape[0]
    T = 512
    NH = FH // T
    NP = pk_own.shape[1]
    tile = lambda t, s: jnp.where(t < NH, s[0] * NH + t, (1 - s[0]) * NH + t - NH)
    first = lambda t: jnp.minimum(t, NH - 1)
    second = lambda t: jnp.maximum(t - NH, 0)
    const = lambda *shape: pl.BlockSpec(shape, lambda t, s: (0,) * len(shape))
    wf = pl.BlockSpec((H, T), lambda t, s: (0, tile(t, s)))
    return call(
        functools.partial(ffn_kernel, T=T), "ffn", (2 * NH,),
        [whole((L, H)), whole((L, H)), whole((L, D)), whole((L, D)), whole((1, NP)), whole((1, NP)), whole((H, D)), whole((H, D)),
         wf, wf, pl.BlockSpec((T, D), lambda t, s: (first(t), 0)), pl.BlockSpec((T, D), lambda t, s: (second(t), 0))],
        [pl.BlockSpec((L, T), lambda t, s: (0, first(t))), pl.BlockSpec((L, T), lambda t, s: (0, second(t))),
         pl.BlockSpec((L, T), lambda t, s: (0, tile(t, s))), const(L, H), const(L, H), const(L, D), const(L, D), const(L, D),
         const(L, H), const(L, H), pl.BlockSpec((8, T), lambda t, s: (0, tile(t, s))), const(8, D)],
        (sds((L, FH), BF), sds((L, FH), BF), sds((L, 2 * FH), BF), sds((L, H), BF), sds((L, H), BF), sds((L, D), BF),
         sds((L, D), F32), sds((L, D), BF), sds((L, H), BF), sds((L, H), BF), sds((8, 2 * FH), F32), sds((8, D), F32)),
        [pltpu.VMEM((L, D), BF), pltpu.VMEM((L, D), F32), pltpu.VMEM((L, D), F32), pltpu.VMEM((L, D), F32),
         pltpu.VMEM((D, T), BF), pltpu.VMEM((T, D), BF), pltpu.VMEM((L, T), BF)],
        cost(2 * L * D * (2 * D + 8 * FH), 24e6, 1.5e6),
        (scal, ak, ar, xb, dz, pk_own, pk_oth, wp_own, wp_oth, wf_own, wf_oth, wo_own, wo_oth),
    )


def pair_of(i, s):
    return ((i + 2) & 3) ^ (s[8] >> 1)


def turns(i, outs):
    return (i == 0, i == 1, i >= 2) if len(outs) == 3 else (i < 2, i >= 2)


def put_pair(scal, left, right, *outs):
    H = left.shape[0]
    i = pl.program_id(0)
    flip = scal[8] & 1
    for out, here in zip(outs, turns(i, outs)):

        @pl.when(here)
        def _():
            out[half(flip, H), :] = left
            out[half(1 - flip, H), :] = right


def pair_specs(H, split):
    block = lambda at: pl.BlockSpec((2 * H, H), lambda i, s: (at(i), 0))
    keep = block(lambda i: jnp.maximum(i - 2, 0))
    if split:
        first = block(lambda i: 0)
        return [first, first, keep], (sds((2 * H, H), BF), sds((2 * H, H), BF), sds((4 * H, H), BF))
    return [block(lambda i: jnp.minimum(i, 1)), keep], (sds((4 * H, H), BF), sds((4 * H, H), BF))


def grad_pair_kernel(scal, a_own, a_oth, b_own, b_oth, *outs):
    H = a_own.shape[1]
    val = (dot_tn(a_own[...], b_own[...]) + dot_tn(a_oth[...], b_oth[...])).astype(BF)
    put_pair(scal, val[:, :H], val[:, H:], *outs)


def grad_rows(scal, a_own, a_oth, b_own, b_oth):
    K, M = a_own.shape
    N = b_own.shape[1]
    H = N // 2
    a = pl.BlockSpec((K, H), lambda i, s: (0, pair_of(i, s)))
    specs, shape = pair_specs(H, False)
    return call(
        grad_pair_kernel, "grad_rows", (4,), [a, a, whole((K, N)), whole((K, N))], specs, shape, [],
        cost(4 * K * M * N, 4 * K * (M + N) + 2 * M * N), (scal, a_own, a_oth, b_own, b_oth),
    )


def grad_cols(scal, a_own, a_oth, b_own, b_oth):
    K, M = a_own.shape
    N = b_own.shape[1]
    b = pl.BlockSpec((K, 2 * M), lambda i, s: (0, pair_of(i, s)))
    specs, shape = pair_specs(M, False)
    return call(
        grad_pair_kernel, "grad_cols", (4,), [whole((K, M)), whole((K, M)), b, b], specs, shape, [],
        cost(4 * K * M * N, 4 * K * (M + N) + 2 * M * N), (scal, a_own, a_oth, b_own, b_oth),
    )


def grad_attn_kernel(scal, n_own, n_oth, a_own, a_oth, gb_own, gb_oth, *refs):
    H = n_own.shape[1]
    shard = scal[0]
    outs = refs[-3:]
    n = (len(refs) - 3) // 4
    l_own, l_oth, r_own, r_oth = [refs[n * j : n * j + n] for j in range(4)]
    w = pair_of(pl.program_id(0), scal)
    flip = scal[8] & 1

    def put(rows, value):
        i = pl.program_id(0)
        for out, here in zip(outs, turns(i, outs)):

            @pl.when(here)
            def _():
                out[half(rows, H), :] = value

    def heads(parts):
        return jnp.concatenate([p[0] for p in parts], axis=1)

    @pl.when(w < 3)
    def _():
        mine = dot_tn(n_own[...], heads(l_own)) + dot_tn(n_oth[...], heads(l_oth))
        put(shard ^ flip, mine.astype(BF))
        theirs = dot_tn(n_own[...], heads(r_own)) + dot_tn(n_oth[...], heads(r_oth))
        put(1 - (shard ^ flip), theirs.astype(BF))

    @pl.when(w == 3)
    def _():
        val = (dot_tn(a_own[...], gb_own[...]) + dot_tn(a_oth[...], gb_oth[...])).astype(BF)
        put(flip, val[:, :H])
        put(1 - flip, val[:, H:])


def grad_attn(scal, normed, n_oth, a_own, a_oth, gb_own, gb_oth, *parts):
    K, H = n_oth.shape
    D = 2 * H
    d = [pl.BlockSpec((1, K, p.shape[2]), lambda i, s: (jnp.minimum(pair_of(i, s), 2), 0, 0)) for p in parts]
    n = pl.BlockSpec((K, H), lambda i, s: (0, s[0]), pipeline_mode=pl.Buffered(1))
    w = whole((K, H))
    specs, shape = pair_specs(H, True)
    return call(
        grad_attn_kernel, "grad_attn", (4,), [n, w, w, w, whole((K, D)), whole((K, D))] + d, specs, shape, [],
        cost(32 * K * H * H, 16e6), (scal, normed, n_oth, a_own, a_oth, gb_own, gb_oth, *parts),
    )


def last_kernel(
    scal, d_own, d_oth, xb, dmid, pk_own, pk_oth, w_own, w_oth, sfc, sums,
    gh, glat, s_keep, s_send, gi, es, ds_, vec, *, L,
):
    r_id = pl.program_id(0)
    shard = scal[0]
    RB, D = xb.shape
    H = D // 2
    FF = sfc.shape[1]
    for j in range(3):
        ds_[:, half(2 * j + shard, H)] = d_own[j]
        ds_[:, half(2 * j + 1 - shard, H)] = d_oth[j]
    d = ds_[...]
    es[:, half(shard, H)] = dot_nt(d, w_own[...])
    es[:, half(1 - shard, H)] = dot_nt(d, w_oth[...])
    gn = es[...]
    x = xb[...].astype(F32)
    cen = x - jnp.mean(x, axis=1, keepdims=True)
    r = lax.rsqrt(jnp.mean(cen * cen, axis=1, keepdims=True) + norm_epsilon)
    n = cen * r
    e = gn * both(pk_own, pk_oth, shard, 0, H)
    gi[...] = dmid[...] + r * (e - jnp.mean(e, axis=1, keepdims=True) - n * jnp.mean(e * n, axis=1, keepdims=True))

    @pl.when(r_id == 0)
    def _():
        glat[...] = jnp.zeros_like(glat)
        vec[...] = jnp.zeros_like(vec)

    row0 = shard * L + r_id * RB
    for c in range(6):
        rel = scal[2 + c] - row0

        @pl.when((rel >= 0) & (rel < RB))
        def _():
            glat[c : c + 1, :] = gi[pl.ds(rel, 1), :]
            gi[pl.ds(rel, 1), :] = jnp.zeros((1, D), F32)

    gh[...] = gi[...].astype(BF)
    vec[0:1, 0:D] += jnp.sum(gn * n, axis=0, keepdims=True)
    vec[1:2, 0:D] += jnp.sum(gn, axis=0, keepdims=True)
    vec[2:3, 0:D] += jnp.sum(ds_[:, 0:D].astype(F32), axis=0, keepdims=True)
    vec[2:3, D : 2 * D] += jnp.sum(ds_[:, 2 * D : 3 * D].astype(F32), axis=0, keepdims=True)

    @pl.when(r_id == pl.num_programs(0) - 1)
    def _():
        for side in range(2):
            owner = shard if side == 0 else 1 - shard
            out = s_keep if side == 0 else s_send
            one = half(owner, H)
            wide = vec[2:3, half(owner, D)]
            fc = sfc[0:1, half(owner, FF // 2)]
            flat = jnp.concatenate(
                [vec[0:1, one], vec[1:2, one], wide, sums[0:1, one], sums[1:2, one], sums[2:3, one], fc, sums[3:4, one]], axis=1
            )
            out[...] = jnp.zeros_like(out)
            for k in range(flat.shape[1] // (2 * D)):
                out[k : k + 1, :] = flat[:, k * 2 * D : (k + 1) * 2 * D]


def last_block(scal, parts, xb, dmid, pk_own, pk_oth, w_own, w_oth, sfc, sums):
    L, D = xb.shape
    H = D // 2
    RB = L // 2
    NP = pk_own.shape[1]
    rows = lambda n: pl.BlockSpec((RB, n), lambda r, s: (r, 0))
    const = lambda *shape: pl.BlockSpec(shape, lambda r, s: (0, 0))
    d = [pl.BlockSpec((3, RB, p.shape[2]), lambda r, s: (0, r, 0)) for p in parts]
    return call(
        functools.partial(last_kernel, L=L), "last_block", (2,),
        d + [rows(D), rows(D), whole((1, NP)), whole((1, NP)), whole((H, 3 * D)), whole((H, 3 * D)), whole(sfc.shape), whole(sums.shape)],
        [rows(D), const(8, D), const(8, 2 * D), const(8, 2 * D)],
        (sds((L, D), BF), sds((8, D), F32), sds((8, 2 * D), F32), sds((8, 2 * D), F32)),
        [pltpu.VMEM((RB, D), F32), pltpu.VMEM((RB, D), F32), pltpu.VMEM((RB, 3 * D), BF), pltpu.VMEM((8, 2 * D), F32)],
        cost(6 * L * D * D, 12e6),
        (scal, *parts, xb, dmid, pk_own, pk_oth, w_own, w_oth, sfc, sums),
    )


def final_kernel(scal, *refs, wide):
    pos = refs[:8]
    outs = refs[8:]
    H = pos[0].shape[1]
    w = pl.program_id(0)
    k = w ^ (scal[8] >> 1)
    flip = scal[8] & 1
    for j in range(4):
        for f in range(2):
            for o, here in enumerate((w < wide, w >= wide) if len(outs) == 2 else (True,)):

                @pl.when((k == j) & (flip == f) & here)
                def _():
                    outs[o][:, :H] = pos[2 * j + f][...].astype(F32)
                    outs[o][:, H:] = pos[2 * j + 1 - f][...].astype(F32)


def final(scal, pos, out_specs, out_shape, wide=4):
    H = pos[0].shape[1]
    return call(
        functools.partial(final_kernel, wide=wide), "final", (4,), [whole((H, H))] * 8, out_specs, out_shape, [],
        cost(8 * H * H, 48 * H * H), (scal, *pos),
    )


def swap(x):
    return lax.ppermute(x, "shard", [(0, 1), (1, 0)])


def hop(x, first, second):
    pairs = []
    for rep in range(16):
        pairs.append((2 * rep, 2 * (rep ^ first)))
        pairs.append((2 * rep + 1, 2 * (rep ^ second) + 1))
    return lax.ppermute(x, ("rep", "shard"), pairs)


def gate(x, *deps):
    return lax.optimization_barrier((x, *deps))[0]


def gated(xs, *deps):
    return list(lax.optimization_barrier((*xs, *deps))[: len(xs)])


def total(*xs):
    return functools.reduce(lambda a, b: a + b, [x.astype(F32) for x in xs]).astype(BF)


class Reduce:
    def __init__(self, *parts):
        *sends, self.keep, self.dims = parts
        self.H = self.keep.shape[1]
        self.r1 = [hop(send, *self.dims[0]) for send in sends]

    def rows(self, x, a, b):
        return x[a * self.H : b * self.H]

    def hop2(self, *deps):
        self.r1[-1] = gate(self.r1[-1], *deps)
        n = self.r1[-1].shape[0] // self.H
        send = total(self.rows(self.keep, 2, 4), self.rows(self.r1[-1], n - 2, n))
        self.r2 = hop(send, *self.dims[1])
        return send

    def hop3(self, *deps):
        self.r1[0], self.r2 = gated((self.r1[0], self.r2), *deps)
        send = total(self.rows(self.keep, 1, 2), self.rows(self.r1[0], 1, 2), self.rows(self.r2, 1, 2))
        self.r3 = hop(send, *self.dims[2])
        return send

    def hop4(self, *deps):
        self.x = total(self.rows(self.keep, 0, 1), self.rows(self.r1[0], 0, 1), self.rows(self.r2, 0, 1), gate(self.r3, *deps))
        self.r4 = hop(self.x, 8, 8)
        return self.x

    def hop5(self, *deps):
        p0 = total(self.x, gate(self.r4, *deps))
        self.pos = [p0] + [None] * 7
        for i in range(3):
            self.pos[1 << i] = hop(p0, *self.dims[2 - i])
        return p0

    def take(self, i, *deps):
        self.pos[i] = gate(self.pos[i], *deps)
        if i == 1:
            self.pos[3] = hop(self.pos[1], *self.dims[1])
        self.pos[4 + i] = hop(self.pos[i], *self.dims[0])
        return self.pos[i]


def pair_device(
    hidden, latents, latent_pos, prefix, ln1_gain, ln1_bias, w_qkv, b_qv, w_proj, b_proj,
    ln2_gain, ln2_bias, w_fc, b_fc, w_out, b_out, cotangent,
):
    _, L, D = hidden.shape
    H = D // 2
    shard = lax.axis_index("shard").astype(jnp.int32)
    rep = lax.axis_index("rep").astype(jnp.int32)
    bit0, bit1, bit2 = rep & 1, (rep >> 1) & 1, (rep >> 2) & 1
    high = jnp.where(shard == 0, bit0, bit1)
    low = jnp.where(shard == 0, bit1, bit0)
    code = high * 4 + bit2 * 2 + low
    dims = ((1, 2), (4, 4), (2, 1))
    lead = lax.broadcasted_iota(jnp.int32, (16,), 0)
    scal = jnp.where(lead == 0, shard, jnp.where(lead == 1, prefix[0], jnp.where(lead == 8, code, 0)))
    scal = lax.dynamic_update_slice(scal, latent_pos[0].astype(jnp.int32), (2,))

    pk_own = pack([ln1_gain, ln1_bias, b_qv, b_proj, ln2_gain, ln2_bias, b_fc, b_out])
    pk_oth = swap(pk_own)
    qkv_oth = swap(w_qkv)
    hid = hidden[0]
    dz = cotangent[0]
    lat = latents[0]

    send, normed, nrm_send, xb = ln_send(scal, hid, lat, pk_own, pk_oth, w_qkv, qkv_oth)
    recv = swap(send)
    keep = own_heads(scal, normed, pk_own, pk_oth, w_qkv, qkv_oth)
    proj_oth, fc_oth, out_oth, nrm_recv, dz_oth = [swap(gate(a, recv, keep)) for a in (w_proj, w_fc, w_out, nrm_send, dz)]
    att_keep, att_send, lse = attn_fwd(scal, keep, recv)
    att_recv = swap(att_send)
    dz_oth, nrm_recv, xb = gated((dz_oth, nrm_recv, xb))
    act_keep, act_send, gp, n2_keep, n2_send, block_out, dmid, gb, ga_keep, ga_send, sfc, sums = ffn(
        scal, att_keep, att_recv, xb, dz, pk_own, pk_oth, w_proj, proj_oth, w_fc, fc_oth, w_out, out_oth
    )
    act_recv = swap(act_send)
    ga_recv = swap(ga_send)
    gp_oth = swap(gate(gp, act_recv))
    n2_recv = swap(gate(n2_send, act_recv))
    gb_oth = swap(gate(gb, act_recv))
    s_out, k_out = grad_rows(scal, act_keep, act_recv, dz, dz_oth)
    r_out = Reduce(s_out, k_out, dims)
    s_fc, k_fc = grad_cols(scal, n2_keep, gate(n2_recv, k_out), gp, gp_oth)
    r_fc = Reduce(s_fc, k_fc, dims)
    d_own, d_oth = attn_bwd(scal, keep, recv, ga_keep, gate(ga_recv, k_fc), att_keep, att_send, lse, 0, H // 128)
    e_own, e_oth = swap(d_oth), swap(d_own)
    tok = r_out.hop2(d_own)
    tok = r_fc.hop2(tok)
    a_c, b_c, k_c = grad_attn(scal, normed, nrm_recv, att_keep, att_send, gb, gb_oth, d_own, d_oth, gate(e_own, tok), e_oth)
    r_c = Reduce(a_c, b_c, k_c, dims)
    tok = r_out.hop3(k_c)
    tok = r_fc.hop3(tok)
    gh, glat, s_keep, s_send = last_block(
        scal, (d_own, gate(e_own, tok)), xb, dmid, pk_own, pk_oth, w_qkv, qkv_oth, sfc, sums
    )
    s_recv = swap(s_send)
    glat_oth = swap(glat)
    r_out.hop4(gh)
    small = s_keep + s_recv
    glat = glat + glat_oth
    r_c.hop2()
    r_fc.hop4()
    r_out.hop5()
    for bits in ((1, 2), (2, 1), (4, 4), (8, 8)):
        small = small + hop(small, *bits)
    r_c.hop3()
    r_fc.hop5()
    r_c.hop4()
    r_c.hop5()
    for i in (1, 2, 3):
        r_out.take(i)
    for i in (1, 2, 3):
        r_fc.take(i)
    g_out = final(scal, r_out.pos, pl.BlockSpec((H, D), lambda w, s: (w, 0)), sds((4 * H, D), F32))
    r_c.take(1)
    r_c.take(2)
    r_c.take(3, g_out, small)
    g_fc = final(scal, gated(r_fc.pos, g_out), pl.BlockSpec((H, D), lambda w, s: (0, w)), sds((H, 4 * D), F32))
    g_qkv, g_proj = final(
        scal, gated(r_c.pos, g_fc), [pl.BlockSpec((H, D), lambda w, s: (0, jnp.minimum(w, 2))), pl.BlockSpec((H, D), lambda w, s: (0, 0))],
        (sds((H, 3 * D), F32), sds((H, D), F32)), 3,
    )
    flat = small[:3].reshape(-1)
    cuts = [0]
    for v in (ln1_gain, ln1_bias, b_qv, b_proj, ln2_gain, ln2_bias, b_fc, b_out):
        cuts.append(cuts[-1] + v.shape[0])
    vecs = [flat[cuts[i] : cuts[i + 1]] for i in range(8)]
    return (
        block_out[None], gh[None], glat[None, :6], vecs[0], vecs[1], g_qkv, vecs[2], g_proj, vecs[3],
        vecs[4], vecs[5], g_fc, vecs[6], g_out, vecs[7],
    )


def layer_norm(values, norm_gain, norm_shift):
    average = jnp.mean(values, axis=-1, keepdims=True)
    centered = values - average
    variance = jnp.mean(centered * centered, axis=-1, keepdims=True)
    return centered * lax.rsqrt(variance + norm_epsilon) * norm_gain + norm_shift


def gelu_tanh(values):
    return (
        0.5
        * values
        * (1.0 + jnp.tanh(gelu_root * (values + gelu_cubic * values * values * values)))
    )


def head_scores(query_one, key_one, query_pos, key_pos, prefix_one, score_scale):
    scores = (
        jnp.einsum("qhe,khe->hqk", query_one, key_one, preferred_element_type=jnp.float32)
        * score_scale
    )
    causal = (key_pos[None, :] <= query_pos[:, None])[None]
    in_prefix = (key_pos < prefix_one)[None, None, :]
    return jnp.where(causal | in_prefix, scores, masked_score)


def per_device(
    hidden,
    latents,
    latent_pos,
    prefix,
    ln1_gain,
    ln1_bias,
    w_qkv,
    b_qv,
    w_proj,
    b_proj,
    ln2_gain,
    ln2_bias,
    w_fc,
    b_fc,
    w_out,
    b_out,
    cotangent,
):
    seq_count, local_len, model_width = hidden.shape
    head_dim = model_width // HEADS
    score_scale = head_dim ** (-0.5)
    row_start = lax.axis_index("shard") * local_len
    gathered = (
        lax.all_gather(ln1_gain, "shard", axis=0, tiled=True),
        lax.all_gather(ln1_bias, "shard", axis=0, tiled=True),
        lax.all_gather(w_qkv, "shard", axis=0, tiled=True),
        lax.all_gather(b_qv, "shard", axis=0, tiled=True),
        lax.all_gather(w_proj, "shard", axis=0, tiled=True),
        lax.all_gather(b_proj, "shard", axis=0, tiled=True),
        lax.all_gather(ln2_gain, "shard", axis=0, tiled=True),
        lax.all_gather(ln2_bias, "shard", axis=0, tiled=True),
        lax.all_gather(w_fc, "shard", axis=0, tiled=True),
        lax.all_gather(b_fc, "shard", axis=0, tiled=True),
        lax.all_gather(w_out, "shard", axis=0, tiled=True),
        lax.all_gather(b_out, "shard", axis=0, tiled=True),
    )
    (
        full_ln1_gain,
        full_ln1_bias,
        full_qkv,
        full_b_qv,
        full_proj,
        full_b_proj,
        full_ln2_gain,
        full_ln2_bias,
        full_fc,
        full_b_fc,
        complete_output,
        full_b_out,
    ) = gathered
    row_ids = row_start + jnp.arange(local_len, dtype=jnp.int32)
    latent_matches = row_ids[None, :, None] == latent_pos[:, None, :]
    positioned_rows = jnp.einsum(
        "ety,eyw->etw",
        latent_matches.astype(jnp.bfloat16),
        latents,
        preferred_element_type=jnp.float32,
    )
    replaced = jnp.any(latent_matches, axis=-1)[..., None]
    block_in = jnp.where(replaced, positioned_rows, hidden.astype(jnp.float32)).reshape(
        -1, model_width
    )
    normed, back_norm_one = jax.vjp(
        layer_norm, block_in, full_ln1_gain.astype(jnp.float32), full_ln1_bias.astype(jnp.float32)
    )
    normed_low = normed.astype(jnp.bfloat16)
    bias_full = jnp.concatenate(
        [
            full_b_qv[:model_width].astype(jnp.float32),
            jnp.zeros((model_width,), jnp.float32),
            full_b_qv[model_width:].astype(jnp.float32),
        ]
    )
    projected = (
        jnp.dot(normed_low, full_qkv, preferred_element_type=jnp.float32) + bias_full
    ).astype(jnp.bfloat16)
    query_heads = projected[:, :model_width].reshape(seq_count, local_len, HEADS, head_dim)
    key_local = projected[:, model_width : 2 * model_width].reshape(
        seq_count, local_len, model_width
    )
    value_local = projected[:, 2 * model_width :].reshape(seq_count, local_len, model_width)
    key_full, value_full = (
        lax.all_gather(key_local, "shard", axis=1, tiled=True),
        lax.all_gather(value_local, "shard", axis=1, tiled=True),
    )
    full_len = key_full.shape[1]
    key_heads = key_full.reshape(seq_count, full_len, HEADS, head_dim)
    value_heads = value_full.reshape(seq_count, full_len, HEADS, head_dim)
    key_pos_all = jnp.arange(full_len, dtype=jnp.int32)

    def forward_seq(items):
        query_one, key_one, value_one, prefix_one = items
        scores = head_scores(query_one, key_one, row_ids, key_pos_all, prefix_one, score_scale)
        row_peak = jnp.max(scores, axis=-1, keepdims=True)
        single_logsumexp = row_peak + jnp.log(
            jnp.sum(jnp.exp(scores - row_peak), axis=-1, keepdims=True)
        )
        probs_low = jnp.exp(scores - single_logsumexp).astype(jnp.bfloat16)
        mixed = jnp.einsum("hqk,khe->qhe", probs_low, value_one, preferred_element_type=jnp.float32)
        return (mixed.astype(jnp.bfloat16), single_logsumexp)

    attended_heads, log_total = lax.map(forward_seq, (query_heads, key_heads, value_heads, prefix))
    attended = attended_heads.reshape(-1, model_width)
    middle = (
        block_in
        + jnp.dot(attended, full_proj, preferred_element_type=jnp.float32)
        + full_b_proj.astype(jnp.float32)
    )
    normed_two, back_norm_two = jax.vjp(
        layer_norm, middle, full_ln2_gain.astype(jnp.float32), full_ln2_bias.astype(jnp.float32)
    )
    normed_two_low = normed_two.astype(jnp.bfloat16)
    pre_act = jnp.dot(
        normed_two_low, full_fc, preferred_element_type=jnp.float32
    ) + full_b_fc.astype(jnp.float32)
    activated, back_gelu = jax.vjp(gelu_tanh, pre_act)
    activated_low = activated.astype(jnp.bfloat16)
    block_out = (
        middle
        + jnp.dot(activated_low, complete_output, preferred_element_type=jnp.float32)
        + full_b_out.astype(jnp.float32)
    )
    block_out = block_out.reshape(seq_count, local_len, model_width).astype(jnp.bfloat16)
    back_qkv, back_proj, back_fc, back_out = (
        lax.all_gather(w_qkv, "shard", axis=0, tiled=True),
        lax.all_gather(w_proj, "shard", axis=0, tiled=True),
        lax.all_gather(w_fc, "shard", axis=0, tiled=True),
        lax.all_gather(w_out, "shard", axis=0, tiled=True),
    )
    grad_top = cotangent.reshape(-1, model_width)
    grad_w_out = jnp.einsum(
        "nf,nd->fd", activated_low, grad_top, preferred_element_type=jnp.float32
    )
    grad_b_out = jnp.sum(grad_top.astype(jnp.float32), axis=0)
    grad_act = jnp.einsum("nd,fd->nf", grad_top, back_out, preferred_element_type=jnp.float32)
    (grad_pre,) = back_gelu(grad_act)
    grad_pre_low = grad_pre.astype(jnp.bfloat16)
    grad_w_fc = jnp.einsum(
        "nd,nf->df", normed_two_low, grad_pre_low, preferred_element_type=jnp.float32
    )
    grad_b_fc = jnp.sum(grad_pre_low.astype(jnp.float32), axis=0)
    grad_normed_two = jnp.einsum(
        "nf,df->nd", grad_pre_low, back_fc, preferred_element_type=jnp.float32
    )
    grad_mid_norm, grad_ln2_gain, grad_ln2_bias = back_norm_two(grad_normed_two)
    grad_mid = grad_top.astype(jnp.float32) + grad_mid_norm
    grad_branch_low = grad_mid.astype(jnp.bfloat16)
    grad_w_proj = jnp.einsum(
        "nd,ne->de", attended, grad_branch_low, preferred_element_type=jnp.float32
    )
    grad_b_proj = jnp.sum(grad_branch_low.astype(jnp.float32), axis=0)
    grad_att = jnp.einsum(
        "ne,de->nd", grad_branch_low, back_proj, preferred_element_type=jnp.float32
    )
    grad_att_low = grad_att.astype(jnp.bfloat16).reshape(seq_count, local_len, HEADS, head_dim)

    def backward_sequence(items):
        query_one, key_one, value_one, prefix_one, single_logsumexp, upstream = items
        scores = head_scores(query_one, key_one, row_ids, key_pos_all, prefix_one, score_scale)
        attn_probs = jnp.exp(scores - single_logsumexp)
        grad_value_one = jnp.einsum(
            "hqk,qhe->khe",
            attn_probs.astype(jnp.bfloat16),
            upstream,
            preferred_element_type=jnp.float32,
        )
        grad_probs = jnp.einsum(
            "qhe,khe->hqk", upstream, value_one, preferred_element_type=jnp.float32
        )
        delta_one = jnp.sum(grad_probs * attn_probs, axis=-1, keepdims=True)
        grad_scores = (attn_probs * (grad_probs - delta_one)).astype(jnp.bfloat16)
        grad_query_one = (
            jnp.einsum("hqk,khe->qhe", grad_scores, key_one, preferred_element_type=jnp.float32)
            * score_scale
        )
        grad_key_one = (
            jnp.einsum("hqk,qhe->khe", grad_scores, query_one, preferred_element_type=jnp.float32)
            * score_scale
        )
        return (
            grad_query_one,
            grad_key_one.reshape(full_len, model_width),
            grad_value_one.reshape(full_len, model_width),
        )

    grad_query, grad_key_all, grad_value_all = lax.map(
        backward_sequence, (query_heads, key_heads, value_heads, prefix, log_total, grad_att_low)
    )
    grad_key_own, grad_value_own = (
        lax.psum_scatter(
            grad_key_all.astype(jnp.bfloat16), "shard", scatter_dimension=1, tiled=True
        ).astype(jnp.float32),
        lax.psum_scatter(
            grad_value_all.astype(jnp.bfloat16), "shard", scatter_dimension=1, tiled=True
        ).astype(jnp.float32),
    )
    grad_query_low = grad_query.reshape(-1, model_width).astype(jnp.bfloat16)
    grad_key_low = grad_key_own.reshape(-1, model_width).astype(jnp.bfloat16)
    grad_value_low = grad_value_own.reshape(-1, model_width).astype(jnp.bfloat16)
    grad_projected = jnp.concatenate([grad_query_low, grad_key_low, grad_value_low], axis=1)
    grad_b_qv = jnp.concatenate(
        [
            jnp.sum(grad_query_low.astype(jnp.float32), axis=0),
            jnp.sum(grad_value_low.astype(jnp.float32), axis=0),
        ]
    )
    grad_w_qkv = jnp.einsum(
        "nd,ne->de", normed_low, grad_projected, preferred_element_type=jnp.float32
    )
    grad_normed = jnp.einsum(
        "ne,de->nd", grad_projected, back_qkv, preferred_element_type=jnp.float32
    )
    grad_in_norm, grad_ln1_gain, grad_ln1_bias = back_norm_one(grad_normed)
    block_gradient = (grad_mid + grad_in_norm).reshape(seq_count, local_len, model_width)
    latent_terms = jnp.einsum(
        "inv,inz->ivz",
        latent_matches.astype(jnp.float32),
        block_gradient,
        precision=lax.Precision.HIGHEST,
    )
    grad_latents = lax.psum(latent_terms, "shard")
    grad_hidden = jnp.where(replaced, 0.0, block_gradient).astype(jnp.bfloat16)
    shares = (
        lax.psum_scatter(
            grad_ln1_gain.astype(jnp.bfloat16), "shard", scatter_dimension=0, tiled=True
        ).astype(jnp.float32),
        lax.psum_scatter(
            grad_ln1_bias.astype(jnp.bfloat16), "shard", scatter_dimension=0, tiled=True
        ).astype(jnp.float32),
        lax.psum_scatter(
            grad_w_qkv.astype(jnp.bfloat16), "shard", scatter_dimension=0, tiled=True
        ).astype(jnp.float32),
        lax.psum_scatter(
            grad_b_qv.astype(jnp.bfloat16), "shard", scatter_dimension=0, tiled=True
        ).astype(jnp.float32),
        lax.psum_scatter(
            grad_w_proj.astype(jnp.bfloat16), "shard", scatter_dimension=0, tiled=True
        ).astype(jnp.float32),
        lax.psum_scatter(
            grad_b_proj.astype(jnp.bfloat16), "shard", scatter_dimension=0, tiled=True
        ).astype(jnp.float32),
        lax.psum_scatter(
            grad_ln2_gain.astype(jnp.bfloat16), "shard", scatter_dimension=0, tiled=True
        ).astype(jnp.float32),
        lax.psum_scatter(
            grad_ln2_bias.astype(jnp.bfloat16), "shard", scatter_dimension=0, tiled=True
        ).astype(jnp.float32),
        lax.psum_scatter(
            grad_w_fc.astype(jnp.bfloat16), "shard", scatter_dimension=0, tiled=True
        ).astype(jnp.float32),
        lax.psum_scatter(
            grad_b_fc.astype(jnp.bfloat16), "shard", scatter_dimension=0, tiled=True
        ).astype(jnp.float32),
        lax.psum_scatter(
            grad_w_out.astype(jnp.bfloat16), "shard", scatter_dimension=0, tiled=True
        ).astype(jnp.float32),
        lax.psum_scatter(
            grad_b_out.astype(jnp.bfloat16), "shard", scatter_dimension=0, tiled=True
        ).astype(jnp.float32),
    )
    summed = (
        lax.psum(shares[0].astype(jnp.bfloat16), "rep").astype(jnp.float32),
        lax.psum(shares[1].astype(jnp.bfloat16), "rep").astype(jnp.float32),
        lax.psum(shares[2].astype(jnp.bfloat16), "rep").astype(jnp.float32),
        lax.psum(shares[3].astype(jnp.bfloat16), "rep").astype(jnp.float32),
        lax.psum(shares[4].astype(jnp.bfloat16), "rep").astype(jnp.float32),
        lax.psum(shares[5].astype(jnp.bfloat16), "rep").astype(jnp.float32),
        lax.psum(shares[6].astype(jnp.bfloat16), "rep").astype(jnp.float32),
        lax.psum(shares[7].astype(jnp.bfloat16), "rep").astype(jnp.float32),
        lax.psum(shares[8].astype(jnp.bfloat16), "rep").astype(jnp.float32),
        lax.psum(shares[9].astype(jnp.bfloat16), "rep").astype(jnp.float32),
        lax.psum(shares[10].astype(jnp.bfloat16), "rep").astype(jnp.float32),
        lax.psum(shares[11].astype(jnp.bfloat16), "rep").astype(jnp.float32),
    )
    (
        total_ln1_gain,
        total_ln1_bias,
        total_w_qkv,
        total_b_qv,
        total_w_proj,
        total_b_proj,
        total_ln2_gain,
        total_ln2_bias,
        total_w_fc,
        total_b_fc,
        total_w_out,
        total_b_out,
    ) = summed
    return (
        block_out,
        grad_hidden,
        grad_latents,
        total_ln1_gain,
        total_ln1_bias,
        total_w_qkv,
        total_b_qv,
        total_w_proj,
        total_b_proj,
        total_ln2_gain,
        total_ln2_bias,
        total_w_fc,
        total_b_fc,
        total_w_out,
        total_b_out,
    )


def solution(mesh):
    sizes = dict(mesh.shape)
    paired = sizes["rep"] == 16 and sizes["shard"] == 2
    body = pair_device if paired else per_device
    in_specs = (
        P("rep", "shard", None),
        P("rep", None, None),
        P("rep", None),
        P("rep"),
        P("shard"),
        P("shard"),
        P("shard", None),
        P("shard"),
        P("shard", None),
        P("shard"),
        P("shard"),
        P("shard"),
        P("shard", None),
        P("shard"),
        P("shard", None),
        P("shard"),
        P("rep", "shard", None),
    )
    out_specs = (
        P("rep", "shard", None),
        P("rep", "shard", None),
        P("rep", None, None),
        P("shard"),
        P("shard"),
        P("shard", None),
        P("shard"),
        P("shard", None),
        P("shard"),
        P("shard"),
        P("shard"),
        P("shard", None),
        P("shard"),
        P("shard", None),
        P("shard"),
    )
    return jax.shard_map(
        body, mesh=mesh, in_specs=in_specs, out_specs=out_specs, check_vma=False
    )
```

profile of v0, /device:TPU:0, one launch (start us, length us, event | category | flops | bytes accessed | tf_op | source)
XLA Modules:
  0.0 215.5 jit_solution(5519556891790006523)
XLA Ops:
  8.1 3.4 %ln_send.1 = (bf16[512,1152]{1,0:T(8,128)(2,1)S(1)}, bf16[512,768]{1,0:T(8,128)(2,1)S(1)}, bf16[512,384]{1,0:T(8,128)(2,1)S(1)}, bf16[512,768]{1,0:T(8,128)(2,1)S(1)}) custom-call(s32[16]{0:T(128)S(1)} %bitcast_dynamic-update-slice_fusion.scal, bf16[512,768]{1,0:T(8,128)(2,1)S(1)} %bitcast.14, bf16[6,768]{1,0:T(8,128)(2,1)S(1)} %bitcast.15, ...), custom_call_target="tpu_custom_call" | custom-call | flops 1 | bytes 1 | tf_op jit(solution)/shard_map/ln_send/pallas_call | solution.py:57
  15.8 11.3 %attn_fwd.1 = (bf16[512,384]{1,0:T(8,128)(2,1)S(1)}, bf16[512,384]{1,0:T(8,128)(2,1)S(1)}, f32[8,1024]{1,0:T(8,128)S(1)}) custom-call(s32[16]{0:T(128)S(1)} %bitcast_dynamic-update-slice_fusion.scal, bf16[512,1152]{1,0:T(8,128)(2,1)S(1)} %own_heads.1.qa.ka.va, bf16[512,1152]{1,0:T(8,128)(2,1)S(1)} %own_heads.1.qa.ka.va, ...), custom_call_target="tpu_custom_call" | custom-call | flops 1 | bytes 1 | tf_op jit(solution)/shard_map/attn_fwd/pallas_call | solution.py:57
  28.9 20.2 %ffn.1 = (bf16[512,1536]{1,0:T(8,128)(2,1)S(1)}, bf16[512,1536]{1,0:T(8,128)(2,1)S(1)}, bf16[512,3072]{1,0:T(8,128)(2,1)S(1)}, bf16[512,384]{1,0:T(8,128)(2,1)S(...) custom-call(s32[16]{0:T(128)S(1)} %bitcast_dynamic-update-slice_fusi, ...), custom_call_target="tpu_custom_call" | custom-call | flops 1 | bytes 1 | tf_op jit(solution)/shard_map/ffn/pallas_call | solution.py:57
  49.5 3.1 %collective-permute-done.10.a_oth = bf16[512,1536]{1,0:T(8,128)(2,1)S(1)} collective-permute-done((bf16[512,1536]{1,0:T(8,128)(2,1)S(1)}, bf16[512,1536]{1,0:T(8,128)(2,1)S(1)}, u32[]{:S(2)}, u32[]{:S(2)}) %collective-permute-start.10) | collective-permute-done | bytes 1572896 | tf_op jit(solution)/shard_map/ppermute | solution.py:678
  53.1 4.5 %grad_rows.1 = (bf16[1536,384]{1,0:T(8,128)(2,1)S(1)}, bf16[1536,384]{1,0:T(8,128)(2,1)S(1)}) custom-call(s32[16]{0:T(128)S(1)} %bitcast_dynamic-update-slice_fusion.scal, bf16[512,1536]{1,0:T(8,128)(2,1)S(1)} %get-tuple-element.109.a_own, bf16[512,1536]{1,0:T(8,128)(2,1)S(1)} %collective-permute-done.10.a_oth, bf16[512,768]{1,0:T(8,128)(2,1)S(1)} %bitcast.13, ...), custom_call_target="tpu_custom_call" | custom-call | flops 1 | bytes 1 | tf_op jit(solution)/shard_map/grad_rows/pallas_call | solution.py:57
  57.6 2.9 %collective-permute-start.15 = (bf16[1536,384]{1,0:T(8,128)(2,1)S(1)}, bf16[1536,384]{1,0:T(8,128)(2,1)S(1)}, u32[]{:S(2)}, u32[]{:S(2)}) collective-permute-start(bf16[1536,384]{1,0:T(8,128)(2,1)S(1)} %get-tuple-element.121), channel_id=1, source_target_pairs={{0,2},{1,5},{2,0},{3,7},{4,6},{5,1},{6,4},{7,3},{8,10},{9,13},{10,... | collective-permute-start | bytes 3538952 | tf_op jit(solution)/shard_map/ppermute | solution.py:686
  60.5 4.6 %grad_cols.1 = (bf16[1536,384]{1,0:T(8,128)(2,1)S(1)}, bf16[1536,384]{1,0:T(8,128)(2,1)S(1)}) custom-call(s32[16]{0:T(128)S(1)} %bitcast_dynamic-update-slice_fusion.scal, bf16[512,384]{1,0:T(8,128)(2,1)S(1)} %get-tuple-element.105.a_own, bf16[512,384]{1,0:T(8,128)(2,1)S(1)} %collective-permute-done.11.a_oth, ...), custom_call_target="tpu_custom_call" | custom-call | flops 1 | bytes 1 | tf_op jit(solution)/shard_map/grad_cols/pallas_call | solution.py:57
  66.5 15.7 %attn_bwd.1 = (bf16[3,512,384]{2,1,0:T(8,128)(2,1)S(1)}, bf16[3,512,384]{2,1,0:T(8,128)(2,1)S(1)}) custom-call(s32[16]{0:T(128)S(1)} %bitcast_dynamic-update-slice_fusion.scal, bf16[512,1152]{1,0:T(8,128)(2,1)S(1)} %own_heads.1.qa.ka.va, bf16[512,1152]{1,0:T(8,128)(2,1)S(1)} %own_heads.1.qa.ka.va, bf16[512,1152]{1,0:T(8,128)(2,1)S(1)} %own_heads.1.qa.ka.va, ...), custom_call_target="tpu_custom_call" | custom-call | flops 1 | bytes 1 | tf_op jit(solution)/shard_map/attn_bwd/pallas_call | solution.py:57
  88.0 5.4 %grad_attn.1 = (bf16[768,384]{1,0:T(8,128)(2,1)S(1)}, bf16[768,384]{1,0:T(8,128)(2,1)S(1)}, bf16[1536,384]{1,0:T(8,128)(2,1)S(1)}) custom-call(s32[16]{0:T(128)S(1)} %bitcast_dynamic-update-slice_fusion.scal, bf16[512,768]{1,0:T(8,128)(2,1)S(1)} %get-tuple-element.90.normed.n_own, bf16[512,384]{1,0:T(8,128)(2,1)S(1)} %collective-permute-done.5.n_oth, ...), custom_call_target="tpu_custom_call" | custom-call | flops 1 | bytes 1 | tf_op jit(solution)/shard_map/grad_attn/pallas_call | solution.py:57
  96.6 3.1 %collective-permute-done.17 = bf16[768,384]{1,0:T(8,128)(2,1)S(1)} collective-permute-done((bf16[768,384]{1,0:T(8,128)(2,1)S(1)}, bf16[768,384]{1,0:T(8,128)(2,1)S(1)}, u32[]{:S(2)}, u32[]{:S(2)}) %collective-permute-start.17) | collective-permute-done | bytes 589856 | tf_op jit(solution)/shard_map/ppermute | solution.py:686
  101.7 4.1 %collective-permute-done.27 = bf16[768,384]{1,0:T(8,128)(2,1)S(1)} collective-permute-done((bf16[768,384]{1,0:T(8,128)(2,1)S(1)}, bf16[768,384]{1,0:T(8,128)(2,1)S(1)}, u32[]{:S(2)}, u32[]{:S(2)}) %collective-permute-start.27) | collective-permute-done | bytes 589856 | tf_op jit(solution)/shard_map/ppermute | solution.py:686
  107.7 4.6 %collective-permute-done.16 = bf16[768,384]{1,0:T(8,128)(2,1)S(1)} collective-permute-done((bf16[768,384]{1,0:T(8,128)(2,1)S(1)}, bf16[768,384]{1,0:T(8,128)(2,1)S(1)}, u32[]{:S(2)}, u32[]{:S(2)}) %collective-permute-start.16) | collective-permute-done | bytes 589856 | tf_op jit(solution)/shard_map/ppermute | solution.py:686
  112.4 6.2 %last_block.1 = (bf16[512,768]{1,0:T(8,128)(2,1)}, f32[8,768]{1,0:T(8,128)S(1)}, f32[8,1536]{1,0:T(8,128)S(1)}, f32[8,1536]{1,0:T(8,128)S(1)}) custom-call(s32[16]{0:T(128)S(1)} %bitcast_dynamic-update-slice_fusion.scal, bf16[3,512,384]{2,1,0:T(8,128)(2,1)S(1)} %get-tuple-element.118.refs_0_.d_own, ...), custom_call_target="tpu_custom_call" | custom-call | flops 1 | bytes 1 | tf_op jit(solution)/shard_map/last_block/pallas_call | solution.py:57
  118.7 2.7 %collective-permute-start.35 = (bf16[384,384]{1,0:T(8,128)(2,1)S(1)}, bf16[384,384]{1,0:T(8,128)(2,1)S(1)}, u32[]{:S(2)}, u32[]{:S(2)}) collective-permute-start(bf16[384,384]{1,0:T(8,128)(2,1)S(1)} %add_convert_fusion.6), channel_id=1, source_target_pairs={{0,16},{1,17},{2,18},{3,19},{4,20},{5,21},{6,22},{7,23},{8,24},{9,... | collective-permute-start | bytes 884744 | tf_op jit(solution)/shard_map/ppermute | solution.py:686
  123.4 10.0 %collective-permute-done.35 = bf16[384,384]{1,0:T(8,128)(2,1)S(1)} collective-permute-done((bf16[384,384]{1,0:T(8,128)(2,1)S(1)}, bf16[384,384]{1,0:T(8,128)(2,1)S(1)}, u32[]{:S(2)}, u32[]{:S(2)}) %collective-permute-start.35) | collective-permute-done | bytes 294944 | tf_op jit(solution)/shard_map/ppermute | solution.py:686
  137.6 4.2 %collective-permute-start.37 = (bf16[384,384]{1,0:T(8,128)(2,1)S(1)}, bf16[384,384]{1,0:T(8,128)(2,1)S(1)}, u32[]{:S(2)}, u32[]{:S(2)}) collective-permute-start(bf16[384,384]{1,0:T(8,128)(2,1)S(1)} %add_convert_fusion.5.refs_0_), channel_id=1, source_target_pairs={{0,8},{1,9},{2,10},{3,11},{4,12},{5,13},{6,14},{7,15},{8,0},{9,1},... | collective-permute-start | bytes 884744 | tf_op jit(solution)/shard_map/ppermute | solution.py:686
  146.2 7.5 %collective-permute-done.48 = bf16[384,384]{1,0:T(8,128)(2,1)S(1)} collective-permute-done((bf16[384,384]{1,0:T(8,128)(2,1)S(1)}, bf16[384,384]{1,0:T(8,128)(2,1)S(1)}, u32[]{:S(2)}, u32[]{:S(2)}) %collective-permute-start.48) | collective-permute-done | bytes 294944 | tf_op jit(solution)/shard_map/ppermute | solution.py:686
  169.6 2.6 %collective-permute-done.31.refs_1_ = bf16[384,384]{1,0:T(8,128)(2,1)S(1)} collective-permute-done((bf16[384,384]{1,0:T(8,128)(2,1)S(1)}, bf16[384,384]{1,0:T(8,128)(2,1)S(1)}, u32[]{:S(2)}, u32[]{:S(2)}) %collective-permute-start.31) | collective-permute-done | bytes 294944 | tf_op jit(solution)/shard_map/ppermute | solution.py:686
  172.1 3.0 %collective-permute-start.32 = (bf16[384,384]{1,0:T(8,128)(2,1)S(1)}, bf16[384,384]{1,0:T(8,128)(2,1)S(1)}, u32[]{:S(2)}, u32[]{:S(2)}) collective-permute-start(bf16[384,384]{1,0:T(8,128)(2,1)S(1)} %add_convert_fusion.7.refs_0_), channel_id=1, source_target_pairs={{0,8},{1,9},{2,10},{3,11},{4,12},{5,13},{6,14},{7,15},{8,0},{9,1},... | collective-permute-start | bytes 884744 | tf_op jit(solution)/shard_map/ppermute | solution.py:686
  181.9 5.4 %collective-permute-done.32.refs_2_ = bf16[384,384]{1,0:T(8,128)(2,1)S(1)} collective-permute-done((bf16[384,384]{1,0:T(8,128)(2,1)S(1)}, bf16[384,384]{1,0:T(8,128)(2,1)S(1)}, u32[]{:S(2)}, u32[]{:S(2)}) %collective-permute-start.32) | collective-permute-done | bytes 294944 | tf_op jit(solution)/shard_map/ppermute | solution.py:686
  187.3 3.2 %final.3 = f32[1536,768]{1,0:T(8,128)} custom-call(s32[16]{0:T(128)S(1)} %bitcast_dynamic-update-slice_fusion.scal, bf16[384,384]{1,0:T(8,128)(2,1)S(1)} %add_convert_fusion.5.refs_0_, bf16[384,384]{1,0:T(8,128)(2,1)S(1)} %collective-permute-done.36.refs_1_, bf16[384,384]{1,0:T(8,128)(2,1)S(1)} %collective-permute-done.37.refs_2_, ...), custom_call_target="tpu_custom_call" | custom-call | flops 1 | bytes 1 | tf_op jit(solution)/shard_map/final/pallas_call | solution.py:57
  202.7 3.2 %final.4 = f32[384,3072]{1,0:T(8,128)} custom-call(s32[16]{0:T(128)S(1)} %bitcast_dynamic-update-slice_fusion.scal, bf16[384,384]{1,0:T(8,128)(2,1)S(1)} %add_convert_fusion.3.refs_0_, bf16[384,384]{1,0:T(8,128)(2,1)S(1)} %collective-permute-done.49.refs_1_, bf16[384,384]{1,0:T(8,128)(2,1)S(1)} %collective-permute-done.50.refs_2_, ...), custom_call_target="tpu_custom_call" | custom-call | flops 1 | bytes 1 | tf_op jit(solution)/shard_map/final/pallas_call | solution.py:57
  207.5 3.2 %collective-permute-done.46.refs_7_ = bf16[384,384]{1,0:T(8,128)(2,1)} collective-permute-done((bf16[384,384]{1,0:T(8,128)(2,1)S(1)}, bf16[384,384]{1,0:T(8,128)(2,1)}, u32[]{:S(2)}, u32[]{:S(2)}) %collective-permute-start.46) | collective-permute-done | bytes 294944 | tf_op jit(solution)/shard_map/ppermute | solution.py:686
  210.7 4.9 %final.5 = (f32[384,2304]{1,0:T(8,128)}, f32[384,768]{1,0:T(8,128)}) custom-call(s32[16]{0:T(128)S(1)} %bitcast_dynamic-update-slice_fusion.scal, bf16[384,384]{1,0:T(8,128)(2,1)S(1)} %add_convert_fusion.7.refs_0_, bf16[384,384]{1,0:T(8,128)(2,1)S(1)} %collective-permute-done.31.refs_1_, bf16[384,384]{1,0:T(8,128)(2,1)S(1)} %collective-permute-done.32.refs_2_, ...), custom_call_target="tpu_custom_call" | custom-call | flops 1 | bytes 1 | tf_op jit(solution)/shard_map/final/pallas_call | solution.py:57
  (144 shorter events, 75.3 us)
Async XLA Ops:
  14.6 14.4 %collective-permute-start.7 = (bf16[384,3072]{1,0:T(8,128)(2,1)S(1)}, bf16[384,3072]{1,0:T(8,128)(2,1)S(1)}, u32[]{:S(2)}, u32[]{:S(2)}) collective-permute-start(bf16[384,3072]{1,0:T(8,128)(2,1)S(1)} %copy-done.3), channel_id=1, source_target_pairs={{0,1},{1,0},{2,3},{3,2},{4,5},{5,4},{6,7},{7,6},{8,9},{9,8},{10,11... | collective-permute-start | bytes 7077896 | tf_op jit(solution)/shard_map/ppermute | solution.py:678
  14.8 14.1 %collective-permute-start.8 = (bf16[1536,768]{1,0:T(8,128)(2,1)S(1)}, bf16[1536,768]{1,0:T(8,128)(2,1)S(1)}, u32[]{:S(2)}, u32[]{:S(2)}) collective-permute-start(bf16[1536,768]{1,0:T(8,128)(2,1)S(1)} %copy-done.4), channel_id=1, source_target_pairs={{0,1},{1,0},{2,3},{3,2},{4,5},{5,4},{6,7},{7,6},{8,9},{9,8},{10,11... | collective-permute-start | bytes 7077896 | tf_op jit(solution)/shard_map/ppermute | solution.py:678
  57.6 25.6 %collective-permute-start.15 = (bf16[1536,384]{1,0:T(8,128)(2,1)S(1)}, bf16[1536,384]{1,0:T(8,128)(2,1)S(1)}, u32[]{:S(2)}, u32[]{:S(2)}) collective-permute-start(bf16[1536,384]{1,0:T(8,128)(2,1)S(1)} %get-tuple-element.121), channel_id=1, source_target_pairs={{0,2},{1,5},{2,0},{3,7},{4,6},{5,1},{6,4},{7,3},{8,10},{9,13},{10,... | collective-permute-start | bytes 3538952 | tf_op jit(solution)/shard_map/ppermute | solution.py:686
  65.1 22.2 %collective-permute-start.14 = (bf16[1536,384]{1,0:T(8,128)(2,1)S(1)}, bf16[1536,384]{1,0:T(8,128)(2,1)S(1)}, u32[]{:S(2)}, u32[]{:S(2)}) collective-permute-start(bf16[1536,384]{1,0:T(8,128)(2,1)S(1)} %get-tuple-element.120), channel_id=1, source_target_pairs={{0,2},{1,5},{2,0},{3,7},{4,6},{5,1},{6,4},{7,3},{8,10},{9,13},{10,... | collective-permute-start | bytes 3538952 | tf_op jit(solution)/shard_map/ppermute | solution.py:686
  83.4 16.3 %collective-permute-start.17 = (bf16[768,384]{1,0:T(8,128)(2,1)S(1)}, bf16[768,384]{1,0:T(8,128)(2,1)S(1)}, u32[]{:S(2)}, u32[]{:S(2)}) collective-permute-start(bf16[768,384]{1,0:T(8,128)(2,1)S(1)} %add_convert_fusion.2), channel_id=1, source_target_pairs={{0,8},{1,9},{2,10},{3,11},{4,12},{5,13},{6,14},{7,15},{8,0},{9,1},... | collective-permute-start | bytes 1769480 | tf_op jit(solution)/shard_map/ppermute | solution.py:686
  95.0 17.3 %collective-permute-start.16 = (bf16[768,384]{1,0:T(8,128)(2,1)S(1)}, bf16[768,384]{1,0:T(8,128)(2,1)S(1)}, u32[]{:S(2)}, u32[]{:S(2)}) collective-permute-start(bf16[768,384]{1,0:T(8,128)(2,1)S(1)} %add_convert_fusion.1), channel_id=1, source_target_pairs={{0,8},{1,9},{2,10},{3,11},{4,12},{5,13},{6,14},{7,15},{8,0},{9,1},... | collective-permute-start | bytes 1769480 | tf_op jit(solution)/shard_map/ppermute | solution.py:686
  99.8 18.8 %collective-permute-start.34 = (bf16[384,384]{1,0:T(8,128)(2,1)S(1)}, bf16[384,384]{1,0:T(8,128)(2,1)S(1)}, u32[]{:S(2)}, u32[]{:S(2)}) collective-permute-start(bf16[384,384]{1,0:T(8,128)(2,1)S(1)} %add_convert_fusion.11), channel_id=1, source_target_pairs={{0,4},{1,3},{2,6},{3,1},{4,0},{5,7},{6,2},{7,5},{8,12},{9,11},{10,... | collective-permute-start | bytes 884744 | tf_op jit(solution)/shard_map/ppermute | solution.py:686
  100.8 32.7 %collective-permute-start.26 = (bf16[768,384]{1,0:T(8,128)(2,1)S(1)}, bf16[768,384]{1,0:T(8,128)(2,1)S(1)}, u32[]{:S(2)}, u32[]{:S(2)}) collective-permute-start(bf16[768,384]{1,0:T(8,128)(2,1)S(1)} %get-tuple-element.141), channel_id=1, source_target_pairs={{0,2},{1,5},{2,0},{3,7},{4,6},{5,1},{6,4},{7,3},{8,10},{9,13},{10,... | collective-permute-start | bytes 1769480 | tf_op jit(solution)/shard_map/ppermute | solution.py:686
  106.0 27.5 %collective-permute-start.28 = (bf16[768,384]{1,0:T(8,128)(2,1)S(1)}, bf16[768,384]{1,0:T(8,128)(2,1)S(1)}, u32[]{:S(2)}, u32[]{:S(2)}) collective-permute-start(bf16[768,384]{1,0:T(8,128)(2,1)S(1)} %add_convert_fusion), channel_id=1, source_target_pairs={{0,8},{1,9},{2,10},{3,11},{4,12},{5,13},{6,14},{7,15},{8,0},{9,1},... | collective-permute-start | bytes 1769480 | tf_op jit(solution)/shard_map/ppermute | solution.py:686
  118.7 14.7 %collective-permute-start.35 = (bf16[384,384]{1,0:T(8,128)(2,1)S(1)}, bf16[384,384]{1,0:T(8,128)(2,1)S(1)}, u32[]{:S(2)}, u32[]{:S(2)}) collective-permute-start(bf16[384,384]{1,0:T(8,128)(2,1)S(1)} %add_convert_fusion.6), channel_id=1, source_target_pairs={{0,16},{1,17},{2,18},{3,19},{4,20},{5,21},{6,22},{7,23},{8,24},{9,... | collective-permute-start | bytes 884744 | tf_op jit(solution)/shard_map/ppermute | solution.py:686
  121.4 14.4 %collective-permute-start.47 = (bf16[384,384]{1,0:T(8,128)(2,1)S(1)}, bf16[384,384]{1,0:T(8,128)(2,1)S(1)}, u32[]{:S(2)}, u32[]{:S(2)}) collective-permute-start(bf16[384,384]{1,0:T(8,128)(2,1)S(1)} %add_convert_fusion.10), channel_id=1, source_target_pairs={{0,4},{1,3},{2,6},{3,1},{4,0},{5,7},{6,2},{7,5},{8,12},{9,11},{10,... | collective-permute-start | bytes 884744 | tf_op jit(solution)/shard_map/ppermute | solution.py:686
  136.0 17.7 %collective-permute-start.48 = (bf16[384,384]{1,0:T(8,128)(2,1)S(1)}, bf16[384,384]{1,0:T(8,128)(2,1)S(1)}, u32[]{:S(2)}, u32[]{:S(2)}) collective-permute-start(bf16[384,384]{1,0:T(8,128)(2,1)S(1)} %add_convert_fusion.4), channel_id=1, source_target_pairs={{0,16},{1,17},{2,18},{3,19},{4,20},{5,21},{6,22},{7,23},{8,24},{9,... | collective-permute-start | bytes 884744 | tf_op jit(solution)/shard_map/ppermute | solution.py:686
  137.6 18.3 %collective-permute-start.37 = (bf16[384,384]{1,0:T(8,128)(2,1)S(1)}, bf16[384,384]{1,0:T(8,128)(2,1)S(1)}, u32[]{:S(2)}, u32[]{:S(2)}) collective-permute-start(bf16[384,384]{1,0:T(8,128)(2,1)S(1)} %add_convert_fusion.5.refs_0_), channel_id=1, source_target_pairs={{0,8},{1,9},{2,10},{3,11},{4,12},{5,13},{6,14},{7,15},{8,0},{9,1},... | collective-permute-start | bytes 884744 | tf_op jit(solution)/shard_map/ppermute | solution.py:686
  142.0 19.0 %collective-permute-start.30 = (bf16[384,384]{1,0:T(8,128)(2,1)S(1)}, bf16[384,384]{1,0:T(8,128)(2,1)S(1)}, u32[]{:S(2)}, u32[]{:S(2)}) collective-permute-start(bf16[384,384]{1,0:T(8,128)(2,1)S(1)} %add_convert_fusion.8), channel_id=1, source_target_pairs={{0,16},{1,17},{2,18},{3,19},{4,20},{5,21},{6,22},{7,23},{8,24},{9,... | collective-permute-start | bytes 884744 | tf_op jit(solution)/shard_map/ppermute | solution.py:686
  144.1 13.7 %collective-permute-start.24 = (f32[8,1536]{1,0:T(8,128)S(1)}, f32[8,1536]{1,0:T(8,128)S(1)}, u32[]{:S(2)}, u32[]{:S(2)}) collective-permute-start(f32[8,1536]{1,0:T(8,128)S(1)} %add.142), channel_id=1, source_target_pairs={{0,8},{1,9},{2,10},{3,11},{4,12},{5,13},{6,14},{7,15},{8,0},{9,1},... | collective-permute-start | bytes 147464 | tf_op jit(solution)/shard_map/ppermute | solution.py:686
  144.9 18.0 %collective-permute-start.38 = (bf16[384,384]{1,0:T(8,128)(2,1)S(1)}, bf16[384,384]{1,0:T(8,128)(2,1)S(1)}, u32[]{:S(2)}, u32[]{:S(2)}) collective-permute-start(bf16[384,384]{1,0:T(8,128)(2,1)S(1)} %collective-permute-done.36.refs_1_), channel_id=1, source_target_pairs={{0,8},{1,9},{2,10},{3,11},{4,12},{5,13},{6,14},{7,15},{8,0},{9,1},... | collective-permute-start | bytes 884744 | tf_op jit(solution)/shard_map/ppermute | solution.py:686
  172.1 15.2 %collective-permute-start.32 = (bf16[384,384]{1,0:T(8,128)(2,1)S(1)}, bf16[384,384]{1,0:T(8,128)(2,1)S(1)}, u32[]{:S(2)}, u32[]{:S(2)}) collective-permute-start(bf16[384,384]{1,0:T(8,128)(2,1)S(1)} %add_convert_fusion.7.refs_0_), channel_id=1, source_target_pairs={{0,8},{1,9},{2,10},{3,11},{4,12},{5,13},{6,14},{7,15},{8,0},{9,1},... | collective-permute-start | bytes 884744 | tf_op jit(solution)/shard_map/ppermute | solution.py:686
  175.1 16.1 %collective-permute-start.33 = (bf16[384,384]{1,0:T(8,128)(2,1)S(1)}, bf16[384,384]{1,0:T(8,128)(2,1)S(1)}, u32[]{:S(2)}, u32[]{:S(2)}) collective-permute-start(bf16[384,384]{1,0:T(8,128)(2,1)S(1)} %collective-permute-done.31.refs_1_), channel_id=1, source_target_pairs={{0,8},{1,9},{2,10},{3,11},{4,12},{5,13},{6,14},{7,15},{8,0},{9,1},... | collective-permute-start | bytes 884744 | tf_op jit(solution)/shard_map/ppermute | solution.py:686
  176.7 16.5 %collective-permute-start.52 = (bf16[384,384]{1,0:T(8,128)(2,1)S(1)}, bf16[384,384]{1,0:T(8,128)(2,1)S(1)}, u32[]{:S(2)}, u32[]{:S(2)}) collective-permute-start(bf16[384,384]{1,0:T(8,128)(2,1)S(1)} %add_convert_fusion.3.refs_0_), channel_id=1, source_target_pairs={{0,2},{1,5},{2,0},{3,7},{4,6},{5,1},{6,4},{7,3},{8,10},{9,13},{10,... | collective-permute-start | bytes 884744 | tf_op jit(solution)/shard_map/ppermute | solution.py:686
  177.6 16.4 %collective-permute-start.54 = (bf16[384,384]{1,0:T(8,128)(2,1)S(1)}, bf16[384,384]{1,0:T(8,128)(2,1)S(1)}, u32[]{:S(2)}, u32[]{:S(2)}) collective-permute-start(bf16[384,384]{1,0:T(8,128)(2,1)S(1)} %collective-permute-done.50.refs_2_), channel_id=1, source_target_pairs={{0,2},{1,5},{2,0},{3,7},{4,6},{5,1},{6,4},{7,3},{8,10},{9,13},{10,... | collective-permute-start | bytes 884744 | tf_op jit(solution)/shard_map/ppermute | solution.py:686
  181.0 14.3 %collective-permute-start.53 = (bf16[384,384]{1,0:T(8,128)(2,1)S(1)}, bf16[384,384]{1,0:T(8,128)(2,1)S(1)}, u32[]{:S(2)}, u32[]{:S(2)}) collective-permute-start(bf16[384,384]{1,0:T(8,128)(2,1)S(1)} %collective-permute-done.49.refs_1_), channel_id=1, source_target_pairs={{0,2},{1,5},{2,0},{3,7},{4,6},{5,1},{6,4},{7,3},{8,10},{9,13},{10,... | collective-permute-start | bytes 884744 | tf_op jit(solution)/shard_map/ppermute | solution.py:686
  191.2 14.6 %collective-permute-start.43 = (bf16[384,384]{1,0:T(8,128)(2,1)S(1)}, bf16[384,384]{1,0:T(8,128)(2,1)}, u32[]{:S(2)}, u32[]{:S(2)}) collective-permute-start(bf16[384,384]{1,0:T(8,128)(2,1)S(1)} %add_convert_fusion.7.refs_0_), channel_id=1, source_target_pairs={{0,2},{1,5},{2,0},{3,7},{4,6},{5,1},{6,4},{7,3},{8,10},{9,13},{10,... | collective-permute-start | bytes 884744 | tf_op jit(solution)/shard_map/ppermute | solution.py:686
  193.2 14.3 %collective-permute-start.44 = (bf16[384,384]{1,0:T(8,128)(2,1)S(1)}, bf16[384,384]{1,0:T(8,128)(2,1)}, u32[]{:S(2)}, u32[]{:S(2)}) collective-permute-start(bf16[384,384]{1,0:T(8,128)(2,1)S(1)} %collective-permute-done.31.refs_1_), channel_id=1, source_target_pairs={{0,2},{1,5},{2,0},{3,7},{4,6},{5,1},{6,4},{7,3},{8,10},{9,13},{10,... | collective-permute-start | bytes 884744 | tf_op jit(solution)/shard_map/ppermute | solution.py:686
  195.3 15.4 %collective-permute-start.46 = (bf16[384,384]{1,0:T(8,128)(2,1)S(1)}, bf16[384,384]{1,0:T(8,128)(2,1)}, u32[]{:S(2)}, u32[]{:S(2)}) collective-permute-start(bf16[384,384]{1,0:T(8,128)(2,1)S(1)} %collective-permute-done.33.refs_3_), channel_id=1, source_target_pairs={{0,2},{1,5},{2,0},{3,7},{4,6},{5,1},{6,4},{7,3},{8,10},{9,13},{10,... | collective-permute-start | bytes 884744 | tf_op jit(solution)/shard_map/ppermute | solution.py:686
  (40 other events, 282.4 us)
where the time goes:
time: 216 us
  Pallas kernels  85.1 us (39%)
  waiting for transfers between devices  59.6 us (28%)
  starting transfers between devices  56.3 us (26%)
  local copies, waits for them, and re-layouts  10.7 us (5%)
  other arithmetic  2.36 us (1%)
    pallas_call x12, Pallas kernels, call(): pl.pallas_call(kernel, out_shape=out_shape, grid_spec=pltpu.PrefetchScala...  85.1 us
    ppermute x38, waiting for transfers between devices, hop(): return lax.ppermute(x, ('rep', 'shard'), pairs)  53.1 us
    ppermute x38, starting transfers between devices, hop(): return lax.ppermute(x, ('rep', 'shard'), pairs)  51.8 us
    ppermute x18, waiting for transfers between devices, swap(): return lax.ppermute(x, 'shard', [(0, 1), (1, 0)])  6.52 us
    ppermute x18, starting transfers between devices, swap(): return lax.ppermute(x, 'shard', [(0, 1), (1, 0)])  4.52 us
  transfers between devices with their start and end apart: 56, of which 22 were waited for; matrix products, arithmetic and copies ran while one was open for 4% of the time, Pallas kernels for 26%

commit v1 on v0

--- a/solution.py
+++ b/solution.py
@@ -674,6 +674,30 @@
     )
 
 
+def unpack_kernel(a, b, *outs):
+    W = a.shape[1]
+    at = 0
+    for out in outs:
+        n = out.shape[0]
+        done = 0
+        while done < n:
+            row, col = divmod(at + done, W)
+            w = min(n - done, W - col)
+            out[done : done + w] = (a[row : row + 1, col : col + w] + b[row : row + 1, col : col + w]).reshape(w)
+            done += w
+        at += n
+
+
+def unpack(a, b, sizes):
+    return pl.pallas_call(
+        unpack_kernel,
+        out_shape=[sds((n,), F32) for n in sizes],
+        compiler_params=params(),
+        cost_estimate=cost(1, 1),
+        name="unpack",
+    )(a, b)
+
+
 def swap(x):
     return lax.ppermute(x, "shard", [(0, 1), (1, 0)])
 
@@ -733,6 +757,8 @@
         return p0
 
     def take(self, i, *deps):
+        if i >= 2:
+            deps += (self.pos[2 + i],)
         self.pos[i] = gate(self.pos[i], *deps)
         if i == 1:
             self.pos[3] = hop(self.pos[1], *self.dims[1])
@@ -751,8 +777,8 @@
     bit0, bit1, bit2 = rep & 1, (rep >> 1) & 1, (rep >> 2) & 1
     high = jnp.where(shard == 0, bit0, bit1)
     low = jnp.where(shard == 0, bit1, bit0)
-    code = high * 4 + bit2 * 2 + low
-    dims = ((1, 2), (4, 4), (2, 1))
+    code = high * 4 + low * 2 + bit2
+    dims = ((1, 2), (2, 1), (4, 4))
     lead = lax.broadcasted_iota(jnp.int32, (16,), 0)
     scal = jnp.where(lead == 0, shard, jnp.where(lead == 1, prefix[0], jnp.where(lead == 8, code, 0)))
     scal = lax.dynamic_update_slice(scal, latent_pos[0].astype(jnp.int32), (2,))
@@ -790,42 +816,41 @@
     a_c, b_c, k_c = grad_attn(scal, normed, nrm_recv, att_keep, att_send, gb, gb_oth, d_own, d_oth, gate(e_own, tok), e_oth)
     r_c = Reduce(a_c, b_c, k_c, dims)
     tok = r_out.hop3(k_c)
+    tok = r_out.hop4(tok)
     tok = r_fc.hop3(tok)
     gh, glat, s_keep, s_send = last_block(
         scal, (d_own, gate(e_own, tok)), xb, dmid, pk_own, pk_oth, w_qkv, qkv_oth, sfc, sums
     )
     s_recv = swap(s_send)
     glat_oth = swap(glat)
-    r_out.hop4(gh)
-    small = s_keep + s_recv
-    glat = glat + glat_oth
-    r_c.hop2()
-    r_fc.hop4()
-    r_out.hop5()
-    for bits in ((1, 2), (2, 1), (4, 4), (8, 8)):
+    tok = r_c.hop2(gh)
+    tok = r_fc.hop4(tok)
+    tok = r_c.hop3(tok)
+    tok = r_out.hop5(tok)
+    tok = r_c.hop4(tok)
+    tok = r_fc.hop5(tok)
+    small = s_keep + gate(s_recv, tok)
+    glat = glat + gate(glat_oth, tok)
+    for bits in ((1, 2), (2, 1), (4, 4)):
         small = small + hop(small, *bits)
-    r_c.hop3()
-    r_fc.hop5()
-    r_c.hop4()
-    r_c.hop5()
+    m = hop(small, 8, 8)
+    r_c.hop5(tok)
     for i in (1, 2, 3):
         r_out.take(i)
-    for i in (1, 2, 3):
-        r_fc.take(i)
+    r_fc.take(1, r_out.pos[4], r_out.pos[5])
+    r_fc.take(2, r_out.pos[6])
+    r_fc.take(3, r_out.pos[7])
+    r_c.take(1, r_fc.pos[4], r_fc.pos[5])
     g_out = final(scal, r_out.pos, pl.BlockSpec((H, D), lambda w, s: (w, 0)), sds((4 * H, D), F32))
-    r_c.take(1)
-    r_c.take(2)
-    r_c.take(3, g_out, small)
-    g_fc = final(scal, gated(r_fc.pos, g_out), pl.BlockSpec((H, D), lambda w, s: (0, w)), sds((H, 4 * D), F32))
+    r_c.take(2, r_fc.pos[6], g_out)
+    tok = r_c.take(3, r_fc.pos[7])
+    g_fc = final(scal, gated(r_fc.pos, tok), pl.BlockSpec((H, D), lambda w, s: (0, w)), sds((H, 4 * D), F32))
     g_qkv, g_proj = final(
         scal, gated(r_c.pos, g_fc), [pl.BlockSpec((H, D), lambda w, s: (0, jnp.minimum(w, 2))), pl.BlockSpec((H, D), lambda w, s: (0, 0))],
         (sds((H, 3 * D), F32), sds((H, D), F32)), 3,
     )
-    flat = small[:3].reshape(-1)
-    cuts = [0]
-    for v in (ln1_gain, ln1_bias, b_qv, b_proj, ln2_gain, ln2_bias, b_fc, b_out):
-        cuts.append(cuts[-1] + v.shape[0])
-    vecs = [flat[cuts[i] : cuts[i + 1]] for i in range(8)]
+    sizes = [v.shape[0] for v in (ln1_gain, ln1_bias, b_qv, b_proj, ln2_gain, ln2_bias, b_fc, b_out)]
+    vecs = unpack(small, gate(m, tok), sizes)
     return (
         block_out[None], gh[None], glat[None, :6], vecs[0], vecs[1], g_qkv, vecs[2], g_proj, vecs[3],
         vecs[4], vecs[5], g_fc, vecs[6], g_out, vecs[7],

time: 216 us -> 211 us (0.977)
  local copies, waits for them, and re-layouts: 10.7 us -> 4.71 us
  waiting for transfers between devices: 59.6 us -> 61.9 us
    slice x4 -> x0, local copies, waits for them, and re-layouts: 4.59 us -> none  [the longest x3 3.98 us: pair_device(): vecs = [flat[cuts[i]:cuts[i + 1]] for i in range(8)]]
  transfers between devices with their start and end apart: 56 -> 56, of which waited for: 22 -> 19; matrix products, arithmetic and copies ran while one was open for 4% -> 2% of each run, Pallas kernels for 26% -> 27%
where the time goes in v1:
time: 211 us
  Pallas kernels  84.5 us (40%)
  waiting for transfers between devices  61.9 us (29%)
  starting transfers between devices  56.1 us (27%)
  local copies, waits for them, and re-layouts  4.71 us (2%)
  other arithmetic  2.36 us (1%)
    pallas_call x12, Pallas kernels, call(): pl.pallas_call(kernel, out_shape=out_shape, grid_spec=pltpu.PrefetchScala...  83.8 us
    ppermute x38, waiting for transfers between devices, hop(): return lax.ppermute(x, ('rep', 'shard'), pairs)  53.8 us
    ppermute x38, starting transfers between devices, hop(): return lax.ppermute(x, ('rep', 'shard'), pairs)  51.4 us
    ppermute x18, waiting for transfers between devices, swap(): return lax.ppermute(x, 'shard', [(0, 1), (1, 0)])  8.11 us
    ppermute x18, starting transfers between devices, swap(): return lax.ppermute(x, 'shard', [(0, 1), (1, 0)])  4.72 us
  transfers between devices with their start and end apart: 56, of which 19 were waited for; matrix products, arithmetic and copies ran while one was open for 2% of the time, Pallas kernels for 27%

profile of v1, /device:TPU:0, one launch (start us, length us, event | category | flops | bytes accessed | tf_op | source)
XLA Modules:
  0.0 211.2 jit_solution(14172322888460340673)
XLA Ops:
  8.1 3.4 %ln_send.1 = (bf16[512,1152]{1,0:T(8,128)(2,1)S(1)}, bf16[512,768]{1,0:T(8,128)(2,1)S(1)}, bf16[512,384]{1,0:T(8,128)(2,1)S(1)}, bf16[512,768]{1,0:T(8,128)(2,1)S(1)}) custom-call(s32[16]{0:T(128)S(1)} %bitcast_dynamic-update-slice_fusion.scal, bf16[512,768]{1,0:T(8,128)(2,1)S(1)} %bitcast.14, bf16[6,768]{1,0:T(8,128)(2,1)S(1)} %bitcast.15, ...), custom_call_target="tpu_custom_call" | custom-call | flops 1 | bytes 1 | tf_op jit(solution)/shard_map/ln_send/pallas_call | solution.py:57
  15.8 11.3 %attn_fwd.1 = (bf16[512,384]{1,0:T(8,128)(2,1)S(1)}, bf16[512,384]{1,0:T(8,128)(2,1)S(1)}, f32[8,1024]{1,0:T(8,128)S(1)}) custom-call(s32[16]{0:T(128)S(1)} %bitcast_dynamic-update-slice_fusion.scal, bf16[512,1152]{1,0:T(8,128)(2,1)S(1)} %own_heads.1.qa.ka.va, bf16[512,1152]{1,0:T(8,128)(2,1)S(1)} %own_heads.1.qa.ka.va, ...), custom_call_target="tpu_custom_call" | custom-call | flops 1 | bytes 1 | tf_op jit(solution)/shard_map/attn_fwd/pallas_call | solution.py:57
  29.0 20.2 %ffn.1 = (bf16[512,1536]{1,0:T(8,128)(2,1)S(1)}, bf16[512,1536]{1,0:T(8,128)(2,1)S(1)}, bf16[512,3072]{1,0:T(8,128)(2,1)S(1)}, bf16[512,384]{1,0:T(8,128)(2,1)S(...) custom-call(s32[16]{0:T(128)S(1)} %bitcast_dynamic-update-slice_fusi, ...), custom_call_target="tpu_custom_call" | custom-call | flops 1 | bytes 1 | tf_op jit(solution)/shard_map/ffn/pallas_call | solution.py:57
  49.5 3.1 %collective-permute-done.10.a_oth = bf16[512,1536]{1,0:T(8,128)(2,1)S(1)} collective-permute-done((bf16[512,1536]{1,0:T(8,128)(2,1)S(1)}, bf16[512,1536]{1,0:T(8,128)(2,1)S(1)}, u32[]{:S(2)}, u32[]{:S(2)}) %collective-permute-start.10) | collective-permute-done | bytes 1572896 | tf_op jit(solution)/shard_map/ppermute | solution.py:702
  52.9 4.5 %grad_rows.1 = (bf16[1536,384]{1,0:T(8,128)(2,1)S(1)}, bf16[1536,384]{1,0:T(8,128)(2,1)S(1)}) custom-call(s32[16]{0:T(128)S(1)} %bitcast_dynamic-update-slice_fusion.scal, bf16[512,1536]{1,0:T(8,128)(2,1)S(1)} %get-tuple-element.133.a_own, bf16[512,1536]{1,0:T(8,128)(2,1)S(1)} %collective-permute-done.10.a_oth, bf16[512,768]{1,0:T(8,128)(2,1)S(1)} %bitcast.13, ...), custom_call_target="tpu_custom_call" | custom-call | flops 1 | bytes 1 | tf_op jit(solution)/shard_map/grad_rows/pallas_call | solution.py:57
  57.4 2.7 %collective-permute-start.15 = (bf16[1536,384]{1,0:T(8,128)(2,1)S(1)}, bf16[1536,384]{1,0:T(8,128)(2,1)S(1)}, u32[]{:S(2)}, u32[]{:S(2)}) collective-permute-start(bf16[1536,384]{1,0:T(8,128)(2,1)S(1)} %get-tuple-element.145), channel_id=1, source_target_pairs={{0,2},{1,5},{2,0},{3,7},{4,6},{5,1},{6,4},{7,3},{8,10},{9,13},{10,... | collective-permute-start | bytes 3538952 | tf_op jit(solution)/shard_map/ppermute | solution.py:710
  61.9 4.6 %grad_cols.1 = (bf16[1536,384]{1,0:T(8,128)(2,1)S(1)}, bf16[1536,384]{1,0:T(8,128)(2,1)S(1)}) custom-call(s32[16]{0:T(128)S(1)} %bitcast_dynamic-update-slice_fusion.scal, bf16[512,384]{1,0:T(8,128)(2,1)S(1)} %get-tuple-element.129.a_own, bf16[512,384]{1,0:T(8,128)(2,1)S(1)} %collective-permute-done.11.a_oth, ...), custom_call_target="tpu_custom_call" | custom-call | flops 1 | bytes 1 | tf_op jit(solution)/shard_map/grad_cols/pallas_call | solution.py:57
  67.7 15.7 %attn_bwd.1 = (bf16[3,512,384]{2,1,0:T(8,128)(2,1)S(1)}, bf16[3,512,384]{2,1,0:T(8,128)(2,1)S(1)}) custom-call(s32[16]{0:T(128)S(1)} %bitcast_dynamic-update-slice_fusion.scal, bf16[512,1152]{1,0:T(8,128)(2,1)S(1)} %own_heads.1.qa.ka.va, bf16[512,1152]{1,0:T(8,128)(2,1)S(1)} %own_heads.1.qa.ka.va, bf16[512,1152]{1,0:T(8,128)(2,1)S(1)} %own_heads.1.qa.ka.va, ...), custom_call_target="tpu_custom_call" | custom-call | flops 1 | bytes 1 | tf_op jit(solution)/shard_map/attn_bwd/pallas_call | solution.py:57
  90.1 5.4 %grad_attn.1 = (bf16[768,384]{1,0:T(8,128)(2,1)S(1)}, bf16[768,384]{1,0:T(8,128)(2,1)S(1)}, bf16[1536,384]{1,0:T(8,128)(2,1)S(1)}) custom-call(s32[16]{0:T(128)S(1)} %bitcast_dynamic-update-slice_fusion.scal, bf16[512,768]{1,0:T(8,128)(2,1)S(1)} %get-tuple-element.114.normed.n_own, bf16[512,384]{1,0:T(8,128)(2,1)S(1)} %collective-permute-done.5.n_oth, ...), custom_call_target="tpu_custom_call" | custom-call | flops 1 | bytes 1 | tf_op jit(solution)/shard_map/grad_attn/pallas_call | solution.py:57
  99.2 4.6 %collective-permute-done.20 = bf16[384,384]{1,0:T(8,128)(2,1)S(1)} collective-permute-done((bf16[384,384]{1,0:T(8,128)(2,1)S(1)}, bf16[384,384]{1,0:T(8,128)(2,1)S(1)}, u32[]{:S(2)}, u32[]{:S(2)}) %collective-permute-start.20) | collective-permute-done | bytes 294944 | tf_op jit(solution)/shard_map/ppermute | solution.py:710
  104.2 6.2 %last_block.1 = (bf16[512,768]{1,0:T(8,128)(2,1)}, f32[8,768]{1,0:T(8,128)S(1)}, f32[8,1536]{1,0:T(8,128)S(1)}, f32[8,1536]{1,0:T(8,128)S(1)}) custom-call(s32[16]{0:T(128)S(1)} %bitcast_dynamic-update-slice_fusion.scal, bf16[3,512,384]{2,1,0:T(8,128)(2,1)S(1)} %get-tuple-element.142.refs_0_.d_own, ...), custom_call_target="tpu_custom_call" | custom-call | flops 1 | bytes 1 | tf_op jit(solution)/shard_map/last_block/pallas_call | solution.py:57
  115.5 8.6 %collective-permute-done.22 = bf16[384,384]{1,0:T(8,128)(2,1)S(1)} collective-permute-done((bf16[384,384]{1,0:T(8,128)(2,1)S(1)}, bf16[384,384]{1,0:T(8,128)(2,1)S(1)}, u32[]{:S(2)}, u32[]{:S(2)}) %collective-permute-start.22) | collective-permute-done | bytes 294944 | tf_op jit(solution)/shard_map/ppermute | solution.py:710
  133.1 6.8 %collective-permute-done.39.refs_1_ = bf16[384,384]{1,0:T(8,128)(2,1)S(1)} collective-permute-done((bf16[384,384]{1,0:T(8,128)(2,1)S(1)}, bf16[384,384]{1,0:T(8,128)(2,1)S(1)}, u32[]{:S(2)}, u32[]{:S(2)}) %collective-permute-start.39) | collective-permute-done | bytes 294944 | tf_op jit(solution)/shard_map/ppermute | solution.py:710
  139.9 3.5 %collective-permute-start.44 = (bf16[384,384]{1,0:T(8,128)(2,1)S(1)}, bf16[384,384]{1,0:T(8,128)(2,1)S(1)}, u32[]{:S(2)}, u32[]{:S(2)}) collective-permute-start(bf16[384,384]{1,0:T(8,128)(2,1)S(1)} %collective-permute-done.39.refs_1_), channel_id=1, source_target_pairs={{0,4},{1,3},{2,6},{3,1},{4,0},{5,7},{6,2},{7,5},{8,12},{9,11},{10,... | collective-permute-start | bytes 884744 | tf_op jit(solution)/shard_map/ppermute | solution.py:710
  146.4 4.1 %collective-permute-start.34 = (bf16[384,384]{1,0:T(8,128)(2,1)S(1)}, bf16[384,384]{1,0:T(8,128)(2,1)S(1)}, u32[]{:S(2)}, u32[]{:S(2)}) collective-permute-start(bf16[384,384]{1,0:T(8,128)(2,1)S(1)} %add_convert_fusion.5), channel_id=1, source_target_pairs={{0,16},{1,17},{2,18},{3,19},{4,20},{5,21},{6,22},{7,23},{8,24},{9,... | collective-permute-start | bytes 884744 | tf_op jit(solution)/shard_map/ppermute | solution.py:710
  154.2 5.8 %collective-permute-done.37.refs_1_ = bf16[384,384]{1,0:T(8,128)(2,1)S(1)} collective-permute-done((bf16[384,384]{1,0:T(8,128)(2,1)S(1)}, bf16[384,384]{1,0:T(8,128)(2,1)S(1)}, u32[]{:S(2)}, u32[]{:S(2)}) %collective-permute-start.37) | collective-permute-done | bytes 294944 | tf_op jit(solution)/shard_map/ppermute | solution.py:710
  166.2 6.4 %collective-permute-done.45.refs_7_ = bf16[384,384]{1,0:T(8,128)(2,1)S(1)} collective-permute-done((bf16[384,384]{1,0:T(8,128)(2,1)S(1)}, bf16[384,384]{1,0:T(8,128)(2,1)S(1)}, u32[]{:S(2)}, u32[]{:S(2)}) %collective-permute-start.45) | collective-permute-done | bytes 294944 | tf_op jit(solution)/shard_map/ppermute | solution.py:710
  179.4 3.8 %collective-permute-done.53.refs_4_ = bf16[384,384]{1,0:T(8,128)(2,1)S(1)} collective-permute-done((bf16[384,384]{1,0:T(8,128)(2,1)S(1)}, bf16[384,384]{1,0:T(8,128)(2,1)S(1)}, u32[]{:S(2)}, u32[]{:S(2)}) %collective-permute-start.53) | collective-permute-done | bytes 294944 | tf_op jit(solution)/shard_map/ppermute | solution.py:710
  184.9 3.2 %final.3 = f32[1536,768]{1,0:T(8,128)} custom-call(s32[16]{0:T(128)S(1)} %bitcast_dynamic-update-slice_fusion.scal, bf16[384,384]{1,0:T(8,128)(2,1)S(1)} %add_convert_fusion.6.refs_0_, bf16[384,384]{1,0:T(8,128)(2,1)S(1)} %collective-permute-done.39.refs_1_, bf16[384,384]{1,0:T(8,128)(2,1)S(1)} %collective-permute-done.50.refs_2_, ...), custom_call_target="tpu_custom_call" | custom-call | flops 1 | bytes 1 | tf_op jit(solution)/shard_map/final/pallas_call | solution.py:57
  189.6 4.0 %collective-permute-done.47.refs_5_ = bf16[384,384]{1,0:T(8,128)(2,1)S(1)} collective-permute-done((bf16[384,384]{1,0:T(8,128)(2,1)S(1)}, bf16[384,384]{1,0:T(8,128)(2,1)S(1)}, u32[]{:S(2)}, u32[]{:S(2)}) %collective-permute-start.47) | collective-permute-done | bytes 294944 | tf_op jit(solution)/shard_map/ppermute | solution.py:710
  195.8 2.8 %collective-permute-done.32 = f32[8,1536]{1,0:T(8,128)S(1)} collective-permute-done((f32[8,1536]{1,0:T(8,128)S(1)}, f32[8,1536]{1,0:T(8,128)S(1)}, u32[]{:S(2)}, u32[]{:S(2)}) %collective-permute-start.32) | collective-permute-done | bytes 49184 | tf_op jit(solution)/shard_map/ppermute | solution.py:710
  200.1 3.6 %collective-permute-done.33.b = f32[8,1536]{1,0:T(8,128)S(1)} collective-permute-done((f32[8,1536]{1,0:T(8,128)S(1)}, f32[8,1536]{1,0:T(8,128)S(1)}, u32[]{:S(2)}, u32[]{:S(2)}) %collective-permute-start.33) | collective-permute-done | bytes 49184 | tf_op jit(solution)/shard_map/ppermute | solution.py:710
  204.3 3.2 %final.4 = f32[384,3072]{1,0:T(8,128)} custom-call(s32[16]{0:T(128)S(1)} %bitcast_dynamic-update-slice_fusion.scal, bf16[384,384]{1,0:T(8,128)(2,1)S(1)} %add_convert_fusion.4.refs_0_, bf16[384,384]{1,0:T(8,128)(2,1)S(1)} %collective-permute-done.37.refs_1_, bf16[384,384]{1,0:T(8,128)(2,1)S(1)} %collective-permute-done.49.refs_2_, ...), custom_call_target="tpu_custom_call" | custom-call | flops 1 | bytes 1 | tf_op jit(solution)/shard_map/final/pallas_call | solution.py:57
  207.5 3.6 %final.5 = (f32[384,2304]{1,0:T(8,128)}, f32[384,768]{1,0:T(8,128)}) custom-call(s32[16]{0:T(128)S(1)} %bitcast_dynamic-update-slice_fusion.scal, bf16[384,384]{1,0:T(8,128)(2,1)S(1)} %add_convert_fusion.3.refs_0_, bf16[384,384]{1,0:T(8,128)(2,1)S(1)} %collective-permute-done.35.refs_1_, bf16[384,384]{1,0:T(8,128)(2,1)S(1)} %collective-permute-done.48.refs_2_, ...), custom_call_target="tpu_custom_call" | custom-call | flops 1 | bytes 1 | tf_op jit(solution)/shard_map/final/pallas_call | solution.py:57
  (139 shorter events, 68.5 us)
Async XLA Ops:
  14.6 14.4 %collective-permute-start.7 = (bf16[384,3072]{1,0:T(8,128)(2,1)S(1)}, bf16[384,3072]{1,0:T(8,128)(2,1)S(1)}, u32[]{:S(2)}, u32[]{:S(2)}) collective-permute-start(bf16[384,3072]{1,0:T(8,128)(2,1)S(1)} %copy-done.3), channel_id=1, source_target_pairs={{0,1},{1,0},{2,3},{3,2},{4,5},{5,4},{6,7},{7,6},{8,9},{9,8},{10,11... | collective-permute-start | bytes 7077896 | tf_op jit(solution)/shard_map/ppermute | solution.py:702
  14.8 14.1 %collective-permute-start.8 = (bf16[1536,768]{1,0:T(8,128)(2,1)S(1)}, bf16[1536,768]{1,0:T(8,128)(2,1)S(1)}, u32[]{:S(2)}, u32[]{:S(2)}) collective-permute-start(bf16[1536,768]{1,0:T(8,128)(2,1)S(1)} %copy-done.4), channel_id=1, source_target_pairs={{0,1},{1,0},{2,3},{3,2},{4,5},{5,4},{6,7},{7,6},{8,9},{9,8},{10,11... | collective-permute-start | bytes 7077896 | tf_op jit(solution)/shard_map/ppermute | solution.py:702
  15.7 13.3 %collective-permute-start.6 = (bf16[384,768]{1,0:T(8,128)(2,1)S(1)}, bf16[384,768]{1,0:T(8,128)(2,1)S(1)}, u32[]{:S(2)}, u32[]{:S(2)}) collective-permute-start(bf16[384,768]{1,0:T(8,128)(2,1)S(1)} %copy-done.6), channel_id=1, source_target_pairs={{0,1},{1,0},{2,3},{3,2},{4,5},{5,4},{6,7},{7,6},{8,9},{9,8},{10,11... | collective-permute-start | bytes 1769480 | tf_op jit(solution)/shard_map/ppermute | solution.py:702
  57.4 26.8 %collective-permute-start.15 = (bf16[1536,384]{1,0:T(8,128)(2,1)S(1)}, bf16[1536,384]{1,0:T(8,128)(2,1)S(1)}, u32[]{:S(2)}, u32[]{:S(2)}) collective-permute-start(bf16[1536,384]{1,0:T(8,128)(2,1)S(1)} %get-tuple-element.145), channel_id=1, source_target_pairs={{0,2},{1,5},{2,0},{3,7},{4,6},{5,1},{6,4},{7,3},{8,10},{9,13},{10,... | collective-permute-start | bytes 3538952 | tf_op jit(solution)/shard_map/ppermute | solution.py:710
  66.5 20.8 %collective-permute-start.14 = (bf16[1536,384]{1,0:T(8,128)(2,1)S(1)}, bf16[1536,384]{1,0:T(8,128)(2,1)S(1)}, u32[]{:S(2)}, u32[]{:S(2)}) collective-permute-start(bf16[1536,384]{1,0:T(8,128)(2,1)S(1)} %get-tuple-element.144), channel_id=1, source_target_pairs={{0,2},{1,5},{2,0},{3,7},{4,6},{5,1},{6,4},{7,3},{8,10},{9,13},{10,... | collective-permute-start | bytes 3538952 | tf_op jit(solution)/shard_map/ppermute | solution.py:710
  87.4 16.6 %collective-permute-start.16 = (bf16[768,384]{1,0:T(8,128)(2,1)S(1)}, bf16[768,384]{1,0:T(8,128)(2,1)S(1)}, u32[]{:S(2)}, u32[]{:S(2)}) collective-permute-start(bf16[768,384]{1,0:T(8,128)(2,1)S(1)} %add_convert_fusion.1), channel_id=1, source_target_pairs={{0,4},{1,3},{2,6},{3,1},{4,0},{5,7},{6,2},{7,5},{8,12},{9,11},{10,... | collective-permute-start | bytes 1769480 | tf_op jit(solution)/shard_map/ppermute | solution.py:710
  97.2 13.1 %collective-permute-start.23 = (bf16[768,384]{1,0:T(8,128)(2,1)S(1)}, bf16[768,384]{1,0:T(8,128)(2,1)S(1)}, u32[]{:S(2)}, u32[]{:S(2)}) collective-permute-start(bf16[768,384]{1,0:T(8,128)(2,1)S(1)} %get-tuple-element.164), channel_id=1, source_target_pairs={{0,2},{1,5},{2,0},{3,7},{4,6},{5,1},{6,4},{7,3},{8,10},{9,13},{10,... | collective-permute-start | bytes 1769480 | tf_op jit(solution)/shard_map/ppermute | solution.py:710
  98.7 25.6 %collective-permute-start.25 = (bf16[768,384]{1,0:T(8,128)(2,1)S(1)}, bf16[768,384]{1,0:T(8,128)(2,1)S(1)}, u32[]{:S(2)}, u32[]{:S(2)}) collective-permute-start(bf16[768,384]{1,0:T(8,128)(2,1)S(1)} %get-tuple-element.167), channel_id=1, source_target_pairs={{0,2},{1,5},{2,0},{3,7},{4,6},{5,1},{6,4},{7,3},{8,10},{9,13},{10,... | collective-permute-start | bytes 1769480 | tf_op jit(solution)/shard_map/ppermute | solution.py:710
  110.5 13.8 %collective-permute-start.26 = (bf16[768,384]{1,0:T(8,128)(2,1)S(1)}, bf16[768,384]{1,0:T(8,128)(2,1)S(1)}, u32[]{:S(2)}, u32[]{:S(2)}) collective-permute-start(bf16[768,384]{1,0:T(8,128)(2,1)S(1)} %add_convert_fusion), channel_id=1, source_target_pairs={{0,4},{1,3},{2,6},{3,1},{4,0},{5,7},{6,2},{7,5},{8,12},{9,11},{10,... | collective-permute-start | bytes 1769480 | tf_op jit(solution)/shard_map/ppermute | solution.py:710
  112.9 13.8 %collective-permute-start.28 = (bf16[384,384]{1,0:T(8,128)(2,1)S(1)}, bf16[384,384]{1,0:T(8,128)(2,1)S(1)}, u32[]{:S(2)}, u32[]{:S(2)}) collective-permute-start(bf16[384,384]{1,0:T(8,128)(2,1)S(1)} %add_convert_fusion.10), channel_id=1, source_target_pairs={{0,16},{1,17},{2,18},{3,19},{4,20},{5,21},{6,22},{7,23},{8,24},{9,... | collective-permute-start | bytes 884744 | tf_op jit(solution)/shard_map/ppermute | solution.py:710
  126.8 13.1 %collective-permute-start.39 = (bf16[384,384]{1,0:T(8,128)(2,1)S(1)}, bf16[384,384]{1,0:T(8,128)(2,1)S(1)}, u32[]{:S(2)}, u32[]{:S(2)}) collective-permute-start(bf16[384,384]{1,0:T(8,128)(2,1)S(1)} %add_convert_fusion.6.refs_0_), channel_id=1, source_target_pairs={{0,8},{1,9},{2,10},{3,11},{4,12},{5,13},{6,14},{7,15},{8,0},{9,1},... | collective-permute-start | bytes 884744 | tf_op jit(solution)/shard_map/ppermute | solution.py:710
  127.1 16.6 %collective-permute-start.27 = (bf16[384,384]{1,0:T(8,128)(2,1)S(1)}, bf16[384,384]{1,0:T(8,128)(2,1)S(1)}, u32[]{:S(2)}, u32[]{:S(2)}) collective-permute-start(bf16[384,384]{1,0:T(8,128)(2,1)S(1)} %add_convert_fusion.7), channel_id=1, source_target_pairs={{0,8},{1,9},{2,10},{3,11},{4,12},{5,13},{6,14},{7,15},{8,0},{9,1},... | collective-permute-start | bytes 884744 | tf_op jit(solution)/shard_map/ppermute | solution.py:710
  128.9 17.0 %collective-permute-start.24 = (bf16[384,384]{1,0:T(8,128)(2,1)S(1)}, bf16[384,384]{1,0:T(8,128)(2,1)S(1)}, u32[]{:S(2)}, u32[]{:S(2)}) collective-permute-start(bf16[384,384]{1,0:T(8,128)(2,1)S(1)} %add_convert_fusion.8), channel_id=1, source_target_pairs={{0,16},{1,17},{2,18},{3,19},{4,20},{5,21},{6,22},{7,23},{8,24},{9,... | collective-permute-start | bytes 884744 | tf_op jit(solution)/shard_map/ppermute | solution.py:710
  129.9 16.5 %collective-permute-start.50 = (bf16[384,384]{1,0:T(8,128)(2,1)S(1)}, bf16[384,384]{1,0:T(8,128)(2,1)S(1)}, u32[]{:S(2)}, u32[]{:S(2)}) collective-permute-start(bf16[384,384]{1,0:T(8,128)(2,1)S(1)} %add_convert_fusion.6.refs_0_), channel_id=1, source_target_pairs={{0,4},{1,3},{2,6},{3,1},{4,0},{5,7},{6,2},{7,5},{8,12},{9,11},{10,... | collective-permute-start | bytes 884744 | tf_op jit(solution)/shard_map/ppermute | solution.py:710
  132.2 18.4 %collective-permute-start.38 = (bf16[384,384]{1,0:T(8,128)(2,1)S(1)}, bf16[384,384]{1,0:T(8,128)(2,1)S(1)}, u32[]{:S(2)}, u32[]{:S(2)}) collective-permute-start(bf16[384,384]{1,0:T(8,128)(2,1)S(1)} %add_convert_fusion.6.refs_0_), channel_id=1, source_target_pairs={{0,2},{1,5},{2,0},{3,7},{4,6},{5,1},{6,4},{7,3},{8,10},{9,13},{10,... | collective-permute-start | bytes 884744 | tf_op jit(solution)/shard_map/ppermute | solution.py:710
  146.0 14.0 %collective-permute-start.37 = (bf16[384,384]{1,0:T(8,128)(2,1)S(1)}, bf16[384,384]{1,0:T(8,128)(2,1)S(1)}, u32[]{:S(2)}, u32[]{:S(2)}) collective-permute-start(bf16[384,384]{1,0:T(8,128)(2,1)S(1)} %add_convert_fusion.4.refs_0_), channel_id=1, source_target_pairs={{0,8},{1,9},{2,10},{3,11},{4,12},{5,13},{6,14},{7,15},{8,0},{9,1},... | collective-permute-start | bytes 884744 | tf_op jit(solution)/shard_map/ppermute | solution.py:710
  146.4 15.7 %collective-permute-start.34 = (bf16[384,384]{1,0:T(8,128)(2,1)S(1)}, bf16[384,384]{1,0:T(8,128)(2,1)S(1)}, u32[]{:S(2)}, u32[]{:S(2)}) collective-permute-start(bf16[384,384]{1,0:T(8,128)(2,1)S(1)} %add_convert_fusion.5), channel_id=1, source_target_pairs={{0,16},{1,17},{2,18},{3,19},{4,20},{5,21},{6,22},{7,23},{8,24},{9,... | collective-permute-start | bytes 884744 | tf_op jit(solution)/shard_map/ppermute | solution.py:710
  165.0 13.1 %collective-permute-start.52 = (bf16[384,384]{1,0:T(8,128)(2,1)S(1)}, bf16[384,384]{1,0:T(8,128)(2,1)S(1)}, u32[]{:S(2)}, u32[]{:S(2)}) collective-permute-start(bf16[384,384]{1,0:T(8,128)(2,1)S(1)} %collective-permute-done.49.refs_2_), channel_id=1, source_target_pairs={{0,2},{1,5},{2,0},{3,7},{4,6},{5,1},{6,4},{7,3},{8,10},{9,13},{10,... | collective-permute-start | bytes 884744 | tf_op jit(solution)/shard_map/ppermute | solution.py:710
  174.6 13.5 %collective-permute-start.48 = (bf16[384,384]{1,0:T(8,128)(2,1)S(1)}, bf16[384,384]{1,0:T(8,128)(2,1)S(1)}, u32[]{:S(2)}, u32[]{:S(2)}) collective-permute-start(bf16[384,384]{1,0:T(8,128)(2,1)S(1)} %add_convert_fusion.3.refs_0_), channel_id=1, source_target_pairs={{0,4},{1,3},{2,6},{3,1},{4,0},{5,7},{6,2},{7,5},{8,12},{9,11},{10,... | collective-permute-start | bytes 884744 | tf_op jit(solution)/shard_map/ppermute | solution.py:710
  176.1 13.5 %collective-permute-start.46 = (bf16[384,384]{1,0:T(8,128)(2,1)S(1)}, bf16[384,384]{1,0:T(8,128)(2,1)S(1)}, u32[]{:S(2)}, u32[]{:S(2)}) collective-permute-start(bf16[384,384]{1,0:T(8,128)(2,1)S(1)} %collective-permute-done.43.refs_3_), channel_id=1, source_target_pairs={{0,2},{1,5},{2,0},{3,7},{4,6},{5,1},{6,4},{7,3},{8,10},{9,13},{10,... | collective-permute-start | bytes 884744 | tf_op jit(solution)/shard_map/ppermute | solution.py:710
  177.1 16.5 %collective-permute-start.47 = (bf16[384,384]{1,0:T(8,128)(2,1)S(1)}, bf16[384,384]{1,0:T(8,128)(2,1)S(1)}, u32[]{:S(2)}, u32[]{:S(2)}) collective-permute-start(bf16[384,384]{1,0:T(8,128)(2,1)S(1)} %collective-permute-done.35.refs_1_), channel_id=1, source_target_pairs={{0,2},{1,5},{2,0},{3,7},{4,6},{5,1},{6,4},{7,3},{8,10},{9,13},{10,... | collective-permute-start | bytes 884744 | tf_op jit(solution)/shard_map/ppermute | solution.py:710
  178.1 15.5 %collective-permute-start.42 = (bf16[384,384]{1,0:T(8,128)(2,1)S(1)}, bf16[384,384]{1,0:T(8,128)(2,1)S(1)}, u32[]{:S(2)}, u32[]{:S(2)}) collective-permute-start(bf16[384,384]{1,0:T(8,128)(2,1)S(1)} %collective-permute-done.35.refs_1_), channel_id=1, source_target_pairs={{0,4},{1,3},{2,6},{3,1},{4,0},{5,7},{6,2},{7,5},{8,12},{9,11},{10,... | collective-permute-start | bytes 884744 | tf_op jit(solution)/shard_map/ppermute | solution.py:710
  188.1 19.4 %collective-permute-start.54 = (bf16[384,384]{1,0:T(8,128)(2,1)S(1)}, bf16[384,384]{1,0:T(8,128)(2,1)S(1)}, u32[]{:S(2)}, u32[]{:S(2)}) collective-permute-start(bf16[384,384]{1,0:T(8,128)(2,1)S(1)} %collective-permute-done.48.refs_2_), channel_id=1, source_target_pairs={{0,2},{1,5},{2,0},{3,7},{4,6},{5,1},{6,4},{7,3},{8,10},{9,13},{10,... | collective-permute-start | bytes 884744 | tf_op jit(solution)/shard_map/ppermute | solution.py:710
  193.6 13.9 %collective-permute-start.55 = (bf16[384,384]{1,0:T(8,128)(2,1)S(1)}, bf16[384,384]{1,0:T(8,128)(2,1)S(1)}, u32[]{:S(2)}, u32[]{:S(2)}) collective-permute-start(bf16[384,384]{1,0:T(8,128)(2,1)S(1)} %collective-permute-done.42.refs_3_), channel_id=1, source_target_pairs={{0,2},{1,5},{2,0},{3,7},{4,6},{5,1},{6,4},{7,3},{8,10},{9,13},{10,... | collective-permute-start | bytes 884744 | tf_op jit(solution)/shard_map/ppermute | solution.py:710
  (40 other events, 269.8 us)

commit v2 on v1

--- a/solution.py
+++ b/solution.py
@@ -831,8 +831,10 @@
     tok = r_fc.hop5(tok)
     small = s_keep + gate(s_recv, tok)
     glat = glat + gate(glat_oth, tok)
-    for bits in ((1, 2), (2, 1), (4, 4)):
+    for bits in ((1, 2), (2, 1)):
         small = small + hop(small, *bits)
+    early = small
+    small = small + hop(small, 4, 4)
     m = hop(small, 8, 8)
     r_c.hop5(tok)
     for i in (1, 2, 3):
@@ -842,7 +844,7 @@
     r_fc.take(3, r_out.pos[7])
     r_c.take(1, r_fc.pos[4], r_fc.pos[5])
     g_out = final(scal, r_out.pos, pl.BlockSpec((H, D), lambda w, s: (w, 0)), sds((4 * H, D), F32))
-    r_c.take(2, r_fc.pos[6], g_out)
+    r_c.take(2, r_fc.pos[6], g_out, early)
     tok = r_c.take(3, r_fc.pos[7])
     g_fc = final(scal, gated(r_fc.pos, tok), pl.BlockSpec((H, D), lambda w, s: (0, w)), sds((H, 4 * D), F32))
     g_qkv, g_proj = final(

time: 211 us -> 212 us (level)
  transfers between devices with their start and end apart: 56 -> 56, of which waited for: 19 -> 24; matrix products, arithmetic and copies ran while one was open for 2% -> 2% of each run, Pallas kernels for 27% -> 27%
where the time goes in v2:
time: 212 us
  Pallas kernels  84.5 us (40%)
  waiting for transfers between devices  62.8 us (30%)
  starting transfers between devices  55.8 us (26%)
  local copies, waits for them, and re-layouts  4.71 us (2%)
  other arithmetic  2.36 us (1%)
    pallas_call x12, Pallas kernels, call(): pl.pallas_call(kernel, out_shape=out_shape, grid_spec=pltpu.PrefetchScala...  83.9 us
    ppermute x38, waiting for transfers between devices, hop(): return lax.ppermute(x, ('rep', 'shard'), pairs)  54.7 us
    ppermute x38, starting transfers between devices, hop(): return lax.ppermute(x, ('rep', 'shard'), pairs)  51.1 us
    ppermute x18, waiting for transfers between devices, swap(): return lax.ppermute(x, 'shard', [(0, 1), (1, 0)])  8.12 us
    ppermute x18, starting transfers between devices, swap(): return lax.ppermute(x, 'shard', [(0, 1), (1, 0)])  4.67 us
  transfers between devices with their start and end apart: 56, of which 24 were waited for; matrix products, arithmetic and copies ran while one was open for 2% of the time, Pallas kernels for 27%

profile of v2, /device:TPU:0, one launch (start us, length us, event | category | flops | bytes accessed | tf_op | source)
XLA Modules:
  0.0 211.8 jit_solution(11625931915442770289)
XLA Ops:
  8.1 3.4 %ln_send.1 = (bf16[512,1152]{1,0:T(8,128)(2,1)S(1)}, bf16[512,768]{1,0:T(8,128)(2,1)S(1)}, bf16[512,384]{1,0:T(8,128)(2,1)S(1)}, bf16[512,768]{1,0:T(8,128)(2,1)S(1)}) custom-call(s32[16]{0:T(128)S(1)} %bitcast_dynamic-update-slice_fusion.scal, bf16[512,768]{1,0:T(8,128)(2,1)S(1)} %bitcast.14, bf16[6,768]{1,0:T(8,128)(2,1)S(1)} %bitcast.15, ...), custom_call_target="tpu_custom_call" | custom-call | flops 1 | bytes 1 | tf_op jit(solution)/shard_map/ln_send/pallas_call | solution.py:57
  15.8 11.3 %attn_fwd.1 = (bf16[512,384]{1,0:T(8,128)(2,1)S(1)}, bf16[512,384]{1,0:T(8,128)(2,1)S(1)}, f32[8,1024]{1,0:T(8,128)S(1)}) custom-call(s32[16]{0:T(128)S(1)} %bitcast_dynamic-update-slice_fusion.scal, bf16[512,1152]{1,0:T(8,128)(2,1)S(1)} %own_heads.1.qa.ka.va, bf16[512,1152]{1,0:T(8,128)(2,1)S(1)} %own_heads.1.qa.ka.va, ...), custom_call_target="tpu_custom_call" | custom-call | flops 1 | bytes 1 | tf_op jit(solution)/shard_map/attn_fwd/pallas_call | solution.py:57
  28.9 20.2 %ffn.1 = (bf16[512,1536]{1,0:T(8,128)(2,1)S(1)}, bf16[512,1536]{1,0:T(8,128)(2,1)S(1)}, bf16[512,3072]{1,0:T(8,128)(2,1)S(1)}, bf16[512,384]{1,0:T(8,128)(2,1)S(...) custom-call(s32[16]{0:T(128)S(1)} %bitcast_dynamic-update-slice_fusi, ...), custom_call_target="tpu_custom_call" | custom-call | flops 1 | bytes 1 | tf_op jit(solution)/shard_map/ffn/pallas_call | solution.py:57
  49.5 3.1 %collective-permute-done.10.a_oth = bf16[512,1536]{1,0:T(8,128)(2,1)S(1)} collective-permute-done((bf16[512,1536]{1,0:T(8,128)(2,1)S(1)}, bf16[512,1536]{1,0:T(8,128)(2,1)S(1)}, u32[]{:S(2)}, u32[]{:S(2)}) %collective-permute-start.10) | collective-permute-done | bytes 1572896 | tf_op jit(solution)/shard_map/ppermute | solution.py:702
  52.9 4.5 %grad_rows.1 = (bf16[1536,384]{1,0:T(8,128)(2,1)S(1)}, bf16[1536,384]{1,0:T(8,128)(2,1)S(1)}) custom-call(s32[16]{0:T(128)S(1)} %bitcast_dynamic-update-slice_fusion.scal, bf16[512,1536]{1,0:T(8,128)(2,1)S(1)} %get-tuple-element.133.a_own, bf16[512,1536]{1,0:T(8,128)(2,1)S(1)} %collective-permute-done.10.a_oth, bf16[512,768]{1,0:T(8,128)(2,1)S(1)} %bitcast.13, ...), custom_call_target="tpu_custom_call" | custom-call | flops 1 | bytes 1 | tf_op jit(solution)/shard_map/grad_rows/pallas_call | solution.py:57
  57.4 2.7 %collective-permute-start.15 = (bf16[1536,384]{1,0:T(8,128)(2,1)S(1)}, bf16[1536,384]{1,0:T(8,128)(2,1)S(1)}, u32[]{:S(2)}, u32[]{:S(2)}) collective-permute-start(bf16[1536,384]{1,0:T(8,128)(2,1)S(1)} %get-tuple-element.145), channel_id=1, source_target_pairs={{0,2},{1,5},{2,0},{3,7},{4,6},{5,1},{6,4},{7,3},{8,10},{9,13},{10,... | collective-permute-start | bytes 3538952 | tf_op jit(solution)/shard_map/ppermute | solution.py:710
  61.9 4.6 %grad_cols.1 = (bf16[1536,384]{1,0:T(8,128)(2,1)S(1)}, bf16[1536,384]{1,0:T(8,128)(2,1)S(1)}) custom-call(s32[16]{0:T(128)S(1)} %bitcast_dynamic-update-slice_fusion.scal, bf16[512,384]{1,0:T(8,128)(2,1)S(1)} %get-tuple-element.129.a_own, bf16[512,384]{1,0:T(8,128)(2,1)S(1)} %collective-permute-done.11.a_oth, ...), custom_call_target="tpu_custom_call" | custom-call | flops 1 | bytes 1 | tf_op jit(solution)/shard_map/grad_cols/pallas_call | solution.py:57
  67.7 15.7 %attn_bwd.1 = (bf16[3,512,384]{2,1,0:T(8,128)(2,1)S(1)}, bf16[3,512,384]{2,1,0:T(8,128)(2,1)S(1)}) custom-call(s32[16]{0:T(128)S(1)} %bitcast_dynamic-update-slice_fusion.scal, bf16[512,1152]{1,0:T(8,128)(2,1)S(1)} %own_heads.1.qa.ka.va, bf16[512,1152]{1,0:T(8,128)(2,1)S(1)} %own_heads.1.qa.ka.va, bf16[512,1152]{1,0:T(8,128)(2,1)S(1)} %own_heads.1.qa.ka.va, ...), custom_call_target="tpu_custom_call" | custom-call | flops 1 | bytes 1 | tf_op jit(solution)/shard_map/attn_bwd/pallas_call | solution.py:57
  90.0 5.4 %grad_attn.1 = (bf16[768,384]{1,0:T(8,128)(2,1)S(1)}, bf16[768,384]{1,0:T(8,128)(2,1)S(1)}, bf16[1536,384]{1,0:T(8,128)(2,1)S(1)}) custom-call(s32[16]{0:T(128)S(1)} %bitcast_dynamic-update-slice_fusion.scal, bf16[512,768]{1,0:T(8,128)(2,1)S(1)} %get-tuple-element.114.normed.n_own, bf16[512,384]{1,0:T(8,128)(2,1)S(1)} %collective-permute-done.5.n_oth, ...), custom_call_target="tpu_custom_call" | custom-call | flops 1 | bytes 1 | tf_op jit(solution)/shard_map/grad_attn/pallas_call | solution.py:57
  99.2 4.6 %collective-permute-done.20 = bf16[384,384]{1,0:T(8,128)(2,1)S(1)} collective-permute-done((bf16[384,384]{1,0:T(8,128)(2,1)S(1)}, bf16[384,384]{1,0:T(8,128)(2,1)S(1)}, u32[]{:S(2)}, u32[]{:S(2)}) %collective-permute-start.20) | collective-permute-done | bytes 294944 | tf_op jit(solution)/shard_map/ppermute | solution.py:710
  104.2 6.2 %last_block.1 = (bf16[512,768]{1,0:T(8,128)(2,1)}, f32[8,768]{1,0:T(8,128)S(1)}, f32[8,1536]{1,0:T(8,128)S(1)}, f32[8,1536]{1,0:T(8,128)S(1)}) custom-call(s32[16]{0:T(128)S(1)} %bitcast_dynamic-update-slice_fusion.scal, bf16[3,512,384]{2,1,0:T(8,128)(2,1)S(1)} %get-tuple-element.142.refs_0_.d_own, ...), custom_call_target="tpu_custom_call" | custom-call | flops 1 | bytes 1 | tf_op jit(solution)/shard_map/last_block/pallas_call | solution.py:57
  112.9 2.6 %collective-permute-start.28 = (bf16[384,384]{1,0:T(8,128)(2,1)S(1)}, bf16[384,384]{1,0:T(8,128)(2,1)S(1)}, u32[]{:S(2)}, u32[]{:S(2)}) collective-permute-start(bf16[384,384]{1,0:T(8,128)(2,1)S(1)} %add_convert_fusion.10), channel_id=1, source_target_pairs={{0,16},{1,17},{2,18},{3,19},{4,20},{5,21},{6,22},{7,23},{8,24},{9,... | collective-permute-start | bytes 884744 | tf_op jit(solution)/shard_map/ppermute | solution.py:710
  115.5 8.6 %collective-permute-done.22 = bf16[384,384]{1,0:T(8,128)(2,1)S(1)} collective-permute-done((bf16[384,384]{1,0:T(8,128)(2,1)S(1)}, bf16[384,384]{1,0:T(8,128)(2,1)S(1)}, u32[]{:S(2)}, u32[]{:S(2)}) %collective-permute-start.22) | collective-permute-done | bytes 294944 | tf_op jit(solution)/shard_map/ppermute | solution.py:710
  132.2 7.7 %collective-permute-done.39.refs_1_ = bf16[384,384]{1,0:T(8,128)(2,1)S(1)} collective-permute-done((bf16[384,384]{1,0:T(8,128)(2,1)S(1)}, bf16[384,384]{1,0:T(8,128)(2,1)S(1)}, u32[]{:S(2)}, u32[]{:S(2)}) %collective-permute-start.39) | collective-permute-done | bytes 294944 | tf_op jit(solution)/shard_map/ppermute | solution.py:710
  143.8 3.5 %collective-permute-start.44 = (bf16[384,384]{1,0:T(8,128)(2,1)S(1)}, bf16[384,384]{1,0:T(8,128)(2,1)S(1)}, u32[]{:S(2)}, u32[]{:S(2)}) collective-permute-start(bf16[384,384]{1,0:T(8,128)(2,1)S(1)} %collective-permute-done.39.refs_1_), channel_id=1, source_target_pairs={{0,4},{1,3},{2,6},{3,1},{4,0},{5,7},{6,2},{7,5},{8,12},{9,11},{10,... | collective-permute-start | bytes 884744 | tf_op jit(solution)/shard_map/ppermute | solution.py:710
  148.9 3.3 %collective-permute-start.34 = (bf16[384,384]{1,0:T(8,128)(2,1)S(1)}, bf16[384,384]{1,0:T(8,128)(2,1)S(1)}, u32[]{:S(2)}, u32[]{:S(2)}) collective-permute-start(bf16[384,384]{1,0:T(8,128)(2,1)S(1)} %add_convert_fusion.5), channel_id=1, source_target_pairs={{0,16},{1,17},{2,18},{3,19},{4,20},{5,21},{6,22},{7,23},{8,24},{9,... | collective-permute-start | bytes 884744 | tf_op jit(solution)/shard_map/ppermute | solution.py:710
  168.5 5.9 %collective-permute-done.45.refs_7_ = bf16[384,384]{1,0:T(8,128)(2,1)S(1)} collective-permute-done((bf16[384,384]{1,0:T(8,128)(2,1)S(1)}, bf16[384,384]{1,0:T(8,128)(2,1)S(1)}, u32[]{:S(2)}, u32[]{:S(2)}) %collective-permute-start.45) | collective-permute-done | bytes 294944 | tf_op jit(solution)/shard_map/ppermute | solution.py:710
  181.7 3.2 %final.3 = f32[1536,768]{1,0:T(8,128)} custom-call(s32[16]{0:T(128)S(1)} %bitcast_dynamic-update-slice_fusion.scal, bf16[384,384]{1,0:T(8,128)(2,1)S(1)} %add_convert_fusion.6.refs_0_, bf16[384,384]{1,0:T(8,128)(2,1)S(1)} %collective-permute-done.39.refs_1_, bf16[384,384]{1,0:T(8,128)(2,1)S(1)} %collective-permute-done.50.refs_2_, ...), custom_call_target="tpu_custom_call" | custom-call | flops 1 | bytes 1 | tf_op jit(solution)/shard_map/final/pallas_call | solution.py:57
  187.8 3.0 %collective-permute-done.46.refs_7_ = bf16[384,384]{1,0:T(8,128)(2,1)S(1)} collective-permute-done((bf16[384,384]{1,0:T(8,128)(2,1)S(1)}, bf16[384,384]{1,0:T(8,128)(2,1)S(1)}, u32[]{:S(2)}, u32[]{:S(2)}) %collective-permute-start.46) | collective-permute-done | bytes 294944 | tf_op jit(solution)/shard_map/ppermute | solution.py:710
  190.8 3.2 %collective-permute-done.47.refs_5_ = bf16[384,384]{1,0:T(8,128)(2,1)S(1)} collective-permute-done((bf16[384,384]{1,0:T(8,128)(2,1)S(1)}, bf16[384,384]{1,0:T(8,128)(2,1)S(1)}, u32[]{:S(2)}, u32[]{:S(2)}) %collective-permute-start.47) | collective-permute-done | bytes 294944 | tf_op jit(solution)/shard_map/ppermute | solution.py:710
  196.2 2.9 %collective-permute-done.32 = f32[8,1536]{1,0:T(8,128)S(1)} collective-permute-done((f32[8,1536]{1,0:T(8,128)S(1)}, f32[8,1536]{1,0:T(8,128)S(1)}, u32[]{:S(2)}, u32[]{:S(2)}) %collective-permute-start.32) | collective-permute-done | bytes 49184 | tf_op jit(solution)/shard_map/ppermute | solution.py:710
  200.9 3.4 %collective-permute-done.33.b = f32[8,1536]{1,0:T(8,128)S(1)} collective-permute-done((f32[8,1536]{1,0:T(8,128)S(1)}, f32[8,1536]{1,0:T(8,128)S(1)}, u32[]{:S(2)}, u32[]{:S(2)}) %collective-permute-start.33) | collective-permute-done | bytes 49184 | tf_op jit(solution)/shard_map/ppermute | solution.py:710
  205.0 3.2 %final.4 = f32[384,3072]{1,0:T(8,128)} custom-call(s32[16]{0:T(128)S(1)} %bitcast_dynamic-update-slice_fusion.scal, bf16[384,384]{1,0:T(8,128)(2,1)S(1)} %add_convert_fusion.4.refs_0_, bf16[384,384]{1,0:T(8,128)(2,1)S(1)} %collective-permute-done.37.refs_1_, bf16[384,384]{1,0:T(8,128)(2,1)S(1)} %collective-permute-done.49.refs_2_, ...), custom_call_target="tpu_custom_call" | custom-call | flops 1 | bytes 1 | tf_op jit(solution)/shard_map/final/pallas_call | solution.py:57
  208.2 3.6 %final.5 = (f32[384,2304]{1,0:T(8,128)}, f32[384,768]{1,0:T(8,128)}) custom-call(s32[16]{0:T(128)S(1)} %bitcast_dynamic-update-slice_fusion.scal, bf16[384,384]{1,0:T(8,128)(2,1)S(1)} %add_convert_fusion.3.refs_0_, bf16[384,384]{1,0:T(8,128)(2,1)S(1)} %collective-permute-done.35.refs_1_, bf16[384,384]{1,0:T(8,128)(2,1)S(1)} %collective-permute-done.48.refs_2_, ...), custom_call_target="tpu_custom_call" | custom-call | flops 1 | bytes 1 | tf_op jit(solution)/shard_map/final/pallas_call | solution.py:57
  (139 shorter events, 74.4 us)
Async XLA Ops:
  14.6 14.4 %collective-permute-start.7 = (bf16[384,3072]{1,0:T(8,128)(2,1)S(1)}, bf16[384,3072]{1,0:T(8,128)(2,1)S(1)}, u32[]{:S(2)}, u32[]{:S(2)}) collective-permute-start(bf16[384,3072]{1,0:T(8,128)(2,1)S(1)} %copy-done.3), channel_id=1, source_target_pairs={{0,1},{1,0},{2,3},{3,2},{4,5},{5,4},{6,7},{7,6},{8,9},{9,8},{10,11... | collective-permute-start | bytes 7077896 | tf_op jit(solution)/shard_map/ppermute | solution.py:702
  14.8 14.1 %collective-permute-start.8 = (bf16[1536,768]{1,0:T(8,128)(2,1)S(1)}, bf16[1536,768]{1,0:T(8,128)(2,1)S(1)}, u32[]{:S(2)}, u32[]{:S(2)}) collective-permute-start(bf16[1536,768]{1,0:T(8,128)(2,1)S(1)} %copy-done.4), channel_id=1, source_target_pairs={{0,1},{1,0},{2,3},{3,2},{4,5},{5,4},{6,7},{7,6},{8,9},{9,8},{10,11... | collective-permute-start | bytes 7077896 | tf_op jit(solution)/shard_map/ppermute | solution.py:702
  15.7 13.3 %collective-permute-start.6 = (bf16[384,768]{1,0:T(8,128)(2,1)S(1)}, bf16[384,768]{1,0:T(8,128)(2,1)S(1)}, u32[]{:S(2)}, u32[]{:S(2)}) collective-permute-start(bf16[384,768]{1,0:T(8,128)(2,1)S(1)} %copy-done.6), channel_id=1, source_target_pairs={{0,1},{1,0},{2,3},{3,2},{4,5},{5,4},{6,7},{7,6},{8,9},{9,8},{10,11... | collective-permute-start | bytes 1769480 | tf_op jit(solution)/shard_map/ppermute | solution.py:702
  57.4 26.8 %collective-permute-start.15 = (bf16[1536,384]{1,0:T(8,128)(2,1)S(1)}, bf16[1536,384]{1,0:T(8,128)(2,1)S(1)}, u32[]{:S(2)}, u32[]{:S(2)}) collective-permute-start(bf16[1536,384]{1,0:T(8,128)(2,1)S(1)} %get-tuple-element.145), channel_id=1, source_target_pairs={{0,2},{1,5},{2,0},{3,7},{4,6},{5,1},{6,4},{7,3},{8,10},{9,13},{10,... | collective-permute-start | bytes 3538952 | tf_op jit(solution)/shard_map/ppermute | solution.py:710
  66.5 20.8 %collective-permute-start.14 = (bf16[1536,384]{1,0:T(8,128)(2,1)S(1)}, bf16[1536,384]{1,0:T(8,128)(2,1)S(1)}, u32[]{:S(2)}, u32[]{:S(2)}) collective-permute-start(bf16[1536,384]{1,0:T(8,128)(2,1)S(1)} %get-tuple-element.144), channel_id=1, source_target_pairs={{0,2},{1,5},{2,0},{3,7},{4,6},{5,1},{6,4},{7,3},{8,10},{9,13},{10,... | collective-permute-start | bytes 3538952 | tf_op jit(solution)/shard_map/ppermute | solution.py:710
  87.5 16.6 %collective-permute-start.16 = (bf16[768,384]{1,0:T(8,128)(2,1)S(1)}, bf16[768,384]{1,0:T(8,128)(2,1)S(1)}, u32[]{:S(2)}, u32[]{:S(2)}) collective-permute-start(bf16[768,384]{1,0:T(8,128)(2,1)S(1)} %add_convert_fusion.1), channel_id=1, source_target_pairs={{0,4},{1,3},{2,6},{3,1},{4,0},{5,7},{6,2},{7,5},{8,12},{9,11},{10,... | collective-permute-start | bytes 1769480 | tf_op jit(solution)/shard_map/ppermute | solution.py:710
  97.2 13.1 %collective-permute-start.23 = (bf16[768,384]{1,0:T(8,128)(2,1)S(1)}, bf16[768,384]{1,0:T(8,128)(2,1)S(1)}, u32[]{:S(2)}, u32[]{:S(2)}) collective-permute-start(bf16[768,384]{1,0:T(8,128)(2,1)S(1)} %get-tuple-element.164), channel_id=1, source_target_pairs={{0,2},{1,5},{2,0},{3,7},{4,6},{5,1},{6,4},{7,3},{8,10},{9,13},{10,... | collective-permute-start | bytes 1769480 | tf_op jit(solution)/shard_map/ppermute | solution.py:710
  98.7 25.6 %collective-permute-start.25 = (bf16[768,384]{1,0:T(8,128)(2,1)S(1)}, bf16[768,384]{1,0:T(8,128)(2,1)S(1)}, u32[]{:S(2)}, u32[]{:S(2)}) collective-permute-start(bf16[768,384]{1,0:T(8,128)(2,1)S(1)} %get-tuple-element.167), channel_id=1, source_target_pairs={{0,2},{1,5},{2,0},{3,7},{4,6},{5,1},{6,4},{7,3},{8,10},{9,13},{10,... | collective-permute-start | bytes 1769480 | tf_op jit(solution)/shard_map/ppermute | solution.py:710
  110.5 13.8 %collective-permute-start.26 = (bf16[768,384]{1,0:T(8,128)(2,1)S(1)}, bf16[768,384]{1,0:T(8,128)(2,1)S(1)}, u32[]{:S(2)}, u32[]{:S(2)}) collective-permute-start(bf16[768,384]{1,0:T(8,128)(2,1)S(1)} %add_convert_fusion), channel_id=1, source_target_pairs={{0,4},{1,3},{2,6},{3,1},{4,0},{5,7},{6,2},{7,5},{8,12},{9,11},{10,... | collective-permute-start | bytes 1769480 | tf_op jit(solution)/shard_map/ppermute | solution.py:710
  111.4 12.8 %collective-permute-start.22 = (bf16[384,384]{1,0:T(8,128)(2,1)S(1)}, bf16[384,384]{1,0:T(8,128)(2,1)S(1)}, u32[]{:S(2)}, u32[]{:S(2)}) collective-permute-start(bf16[384,384]{1,0:T(8,128)(2,1)S(1)} %add_convert_fusion.9), channel_id=1, source_target_pairs={{0,8},{1,9},{2,10},{3,11},{4,12},{5,13},{6,14},{7,15},{8,0},{9,1},... | collective-permute-start | bytes 884744 | tf_op jit(solution)/shard_map/ppermute | solution.py:710
  112.9 13.8 %collective-permute-start.28 = (bf16[384,384]{1,0:T(8,128)(2,1)S(1)}, bf16[384,384]{1,0:T(8,128)(2,1)S(1)}, u32[]{:S(2)}, u32[]{:S(2)}) collective-permute-start(bf16[384,384]{1,0:T(8,128)(2,1)S(1)} %add_convert_fusion.10), channel_id=1, source_target_pairs={{0,16},{1,17},{2,18},{3,19},{4,20},{5,21},{6,22},{7,23},{8,24},{9,... | collective-permute-start | bytes 884744 | tf_op jit(solution)/shard_map/ppermute | solution.py:710
  126.8 13.1 %collective-permute-start.39 = (bf16[384,384]{1,0:T(8,128)(2,1)S(1)}, bf16[384,384]{1,0:T(8,128)(2,1)S(1)}, u32[]{:S(2)}, u32[]{:S(2)}) collective-permute-start(bf16[384,384]{1,0:T(8,128)(2,1)S(1)} %add_convert_fusion.6.refs_0_), channel_id=1, source_target_pairs={{0,8},{1,9},{2,10},{3,11},{4,12},{5,13},{6,14},{7,15},{8,0},{9,1},... | collective-permute-start | bytes 884744 | tf_op jit(solution)/shard_map/ppermute | solution.py:710
  127.1 16.7 %collective-permute-start.27 = (bf16[384,384]{1,0:T(8,128)(2,1)S(1)}, bf16[384,384]{1,0:T(8,128)(2,1)S(1)}, u32[]{:S(2)}, u32[]{:S(2)}) collective-permute-start(bf16[384,384]{1,0:T(8,128)(2,1)S(1)} %add_convert_fusion.7), channel_id=1, source_target_pairs={{0,8},{1,9},{2,10},{3,11},{4,12},{5,13},{6,14},{7,15},{8,0},{9,1},... | collective-permute-start | bytes 884744 | tf_op jit(solution)/shard_map/ppermute | solution.py:710
  128.9 18.5 %collective-permute-start.24 = (bf16[384,384]{1,0:T(8,128)(2,1)S(1)}, bf16[384,384]{1,0:T(8,128)(2,1)S(1)}, u32[]{:S(2)}, u32[]{:S(2)}) collective-permute-start(bf16[384,384]{1,0:T(8,128)(2,1)S(1)} %add_convert_fusion.8), channel_id=1, source_target_pairs={{0,16},{1,17},{2,18},{3,19},{4,20},{5,21},{6,22},{7,23},{8,24},{9,... | collective-permute-start | bytes 884744 | tf_op jit(solution)/shard_map/ppermute | solution.py:710
  129.9 22.3 %collective-permute-start.29 = (f32[8,1536]{1,0:T(8,128)S(1)}, f32[8,1536]{1,0:T(8,128)S(1)}, u32[]{:S(2)}, u32[]{:S(2)}) collective-permute-start(f32[8,1536]{1,0:T(8,128)S(1)} %get-tuple-element.175), channel_id=1, source_target_pairs={{0,1},{1,0},{2,3},{3,2},{4,5},{5,4},{6,7},{7,6},{8,9},{9,8},{10,11... | collective-permute-start | bytes 147464 | tf_op jit(solution)/shard_map/ppermute | solution.py:702
  129.9 18.8 %collective-permute-start.50 = (bf16[384,384]{1,0:T(8,128)(2,1)S(1)}, bf16[384,384]{1,0:T(8,128)(2,1)S(1)}, u32[]{:S(2)}, u32[]{:S(2)}) collective-permute-start(bf16[384,384]{1,0:T(8,128)(2,1)S(1)} %add_convert_fusion.6.refs_0_), channel_id=1, source_target_pairs={{0,4},{1,3},{2,6},{3,1},{4,0},{5,7},{6,2},{7,5},{8,12},{9,11},{10,... | collective-permute-start | bytes 884744 | tf_op jit(solution)/shard_map/ppermute | solution.py:710
  148.9 14.0 %collective-permute-start.34 = (bf16[384,384]{1,0:T(8,128)(2,1)S(1)}, bf16[384,384]{1,0:T(8,128)(2,1)S(1)}, u32[]{:S(2)}, u32[]{:S(2)}) collective-permute-start(bf16[384,384]{1,0:T(8,128)(2,1)S(1)} %add_convert_fusion.5), channel_id=1, source_target_pairs={{0,16},{1,17},{2,18},{3,19},{4,20},{5,21},{6,22},{7,23},{8,24},{9,... | collective-permute-start | bytes 884744 | tf_op jit(solution)/shard_map/ppermute | solution.py:710
  162.9 13.0 %collective-permute-start.43 = (bf16[384,384]{1,0:T(8,128)(2,1)S(1)}, bf16[384,384]{1,0:T(8,128)(2,1)S(1)}, u32[]{:S(2)}, u32[]{:S(2)}) collective-permute-start(bf16[384,384]{1,0:T(8,128)(2,1)S(1)} %collective-permute-done.37.refs_1_), channel_id=1, source_target_pairs={{0,4},{1,3},{2,6},{3,1},{4,0},{5,7},{6,2},{7,5},{8,12},{9,11},{10,... | collective-permute-start | bytes 884744 | tf_op jit(solution)/shard_map/ppermute | solution.py:710
  167.5 12.6 %collective-permute-start.52 = (bf16[384,384]{1,0:T(8,128)(2,1)S(1)}, bf16[384,384]{1,0:T(8,128)(2,1)S(1)}, u32[]{:S(2)}, u32[]{:S(2)}) collective-permute-start(bf16[384,384]{1,0:T(8,128)(2,1)S(1)} %collective-permute-done.49.refs_2_), channel_id=1, source_target_pairs={{0,2},{1,5},{2,0},{3,7},{4,6},{5,1},{6,4},{7,3},{8,10},{9,13},{10,... | collective-permute-start | bytes 884744 | tf_op jit(solution)/shard_map/ppermute | solution.py:710
  177.5 13.2 %collective-permute-start.46 = (bf16[384,384]{1,0:T(8,128)(2,1)S(1)}, bf16[384,384]{1,0:T(8,128)(2,1)S(1)}, u32[]{:S(2)}, u32[]{:S(2)}) collective-permute-start(bf16[384,384]{1,0:T(8,128)(2,1)S(1)} %collective-permute-done.43.refs_3_), channel_id=1, source_target_pairs={{0,2},{1,5},{2,0},{3,7},{4,6},{5,1},{6,4},{7,3},{8,10},{9,13},{10,... | collective-permute-start | bytes 884744 | tf_op jit(solution)/shard_map/ppermute | solution.py:710
  179.1 14.9 %collective-permute-start.47 = (bf16[384,384]{1,0:T(8,128)(2,1)S(1)}, bf16[384,384]{1,0:T(8,128)(2,1)S(1)}, u32[]{:S(2)}, u32[]{:S(2)}) collective-permute-start(bf16[384,384]{1,0:T(8,128)(2,1)S(1)} %collective-permute-done.35.refs_1_), channel_id=1, source_target_pairs={{0,2},{1,5},{2,0},{3,7},{4,6},{5,1},{6,4},{7,3},{8,10},{9,13},{10,... | collective-permute-start | bytes 884744 | tf_op jit(solution)/shard_map/ppermute | solution.py:710
  180.1 13.8 %collective-permute-start.42 = (bf16[384,384]{1,0:T(8,128)(2,1)S(1)}, bf16[384,384]{1,0:T(8,128)(2,1)S(1)}, u32[]{:S(2)}, u32[]{:S(2)}) collective-permute-start(bf16[384,384]{1,0:T(8,128)(2,1)S(1)} %collective-permute-done.35.refs_1_), channel_id=1, source_target_pairs={{0,4},{1,3},{2,6},{3,1},{4,0},{5,7},{6,2},{7,5},{8,12},{9,11},{10,... | collective-permute-start | bytes 884744 | tf_op jit(solution)/shard_map/ppermute | solution.py:710
  186.9 21.2 %collective-permute-start.54 = (bf16[384,384]{1,0:T(8,128)(2,1)S(1)}, bf16[384,384]{1,0:T(8,128)(2,1)S(1)}, u32[]{:S(2)}, u32[]{:S(2)}) collective-permute-start(bf16[384,384]{1,0:T(8,128)(2,1)S(1)} %collective-permute-done.48.refs_2_), channel_id=1, source_target_pairs={{0,2},{1,5},{2,0},{3,7},{4,6},{5,1},{6,4},{7,3},{8,10},{9,13},{10,... | collective-permute-start | bytes 884744 | tf_op jit(solution)/shard_map/ppermute | solution.py:710
  193.9 14.2 %collective-permute-start.55 = (bf16[384,384]{1,0:T(8,128)(2,1)S(1)}, bf16[384,384]{1,0:T(8,128)(2,1)S(1)}, u32[]{:S(2)}, u32[]{:S(2)}) collective-permute-start(bf16[384,384]{1,0:T(8,128)(2,1)S(1)} %collective-permute-done.42.refs_3_), channel_id=1, source_target_pairs={{0,2},{1,5},{2,0},{3,7},{4,6},{5,1},{6,4},{7,3},{8,10},{9,13},{10,... | collective-permute-start | bytes 884744 | tf_op jit(solution)/shard_map/ppermute | solution.py:710
  (40 other events, 264.0 us)
